TPU v7x, 256 devices: a whole 4x4x8 slice. The times are simulated.
256 devices in a mesh: row: 16 (over z_lo, x, core), col: 16 (over z_hi, y).
Axes of the slice: x: 4, y: 4, z: 8 (z_hi: 4, z_lo: 2; z = z_hi * 2 + z_lo), core: 2. Of those that a mesh axis runs over, the one named last changes fastest.
Arguments:
- blocks_inverse: bfloat16 [12288, 12288], P('row', 'col'), as said below
- factor_rows: bfloat16 [2, 6144, 256], P(None, 'row'), may hold values from -0.15234375 to 0.15234375
- block_lists: int32 [2, 48], replicated, may hold values from 0 to 95, as said below
- diag_inverse: float32 [2, 256, 256], replicated, as said below
Outputs:
- column_inverse: float32 [2, 12288, 256], P(None, 'row')
- mirror_inverse: float32 [2, 256, 12288], P(None, None, 'col')
- diagonal_inverse: float32 [2, 256, 256], replicated
Inputs may be any that keep to these rules, and one draw needn't show every extreme that they name: blocks_inverse is exactly symmetric and positive definite. block_lists[s, m] is 2 * m or 2 * m + 1. diag_inverse[s] is symmetric.
All inputs are finite; a program needn't handle non-finite values.
Results may differ from a plain program's by a relative error of at most 0.0003.
Values may be sent and summed in bfloat16 or wider, within the bound.
A program may use at most 64 MiB of HBM per device.

v0:
```python
import jax
import jax.numpy as jnp
from jax import lax
from jax.sharding import PartitionSpec as P

BS = 128


def broadcast(x, axis, root):
    mine = lax.axis_index(axis) == root
    return lax.psum(jnp.where(mine, x, jnp.zeros_like(x)), axis)


def pair_bits(block_lists, first_block, block_count):
    local_lists = lax.dynamic_slice_in_dim(block_lists, first_block // 2, block_count // 2, 1)
    pair_first = 2 * (first_block // 2 + jnp.arange(block_count // 2, dtype=jnp.int32))
    return local_lists - pair_first[None, :]


def expand_pairs(packed, bits):
    sup_count = packed.shape[0]
    feature_count = packed.shape[2]
    pairs = bits.shape[1]
    grouped = packed.reshape(sup_count, pairs, 1, BS, feature_count)
    which = (
        bits[:, :, None, None, None] == jnp.arange(2, dtype=jnp.int32)[None, None, :, None, None]
    )
    dense = jnp.where(which, grouped, jnp.zeros((), packed.dtype))
    return dense.reshape(sup_count, pairs * 2 * BS, feature_count)


def compact_pairs(dense, bits):
    sup_count = dense.shape[0]
    feature_count = dense.shape[2]
    pairs = bits.shape[1]
    grouped = dense.reshape(sup_count, pairs, 2, BS, feature_count)
    chosen = jnp.where(bits[:, :, None, None] == 0, grouped[:, :, 0], grouped[:, :, 1])
    return chosen.reshape(sup_count, pairs * BS, feature_count)


def multiply_each(matrix, stacked):
    results = []
    for sup_index in range(stacked.shape[0]):
        results.append(
            jnp.dot(matrix, stacked[sup_index].astype(jnp.float32), precision=lax.Precision.HIGHEST)
        )
    return jnp.stack(results)


def local(blocks_inverse, factor_rows, block_lists, diag_inverse):
    row_index = lax.axis_index("row")
    col_index = lax.axis_index("col")
    row_blocks = blocks_inverse.shape[0] // BS
    col_blocks = blocks_inverse.shape[1] // BS
    row_bits = pair_bits(block_lists, row_index * row_blocks, row_blocks)
    col_bits = pair_bits(block_lists, col_index * col_blocks, col_blocks)
    packed_length = col_blocks // 2 * BS
    root_row = col_index * col_blocks // row_blocks
    gathered = lax.all_gather(factor_rows, "row", axis=1, tiled=True)
    column_packed = lax.dynamic_slice_in_dim(gathered, col_index * packed_length, packed_length, 1)
    column_dense = expand_pairs(column_packed, col_bits)
    blocks_wide = blocks_inverse.astype(jnp.float32)
    products = multiply_each(blocks_wide, column_dense)
    listed_products = compact_pairs(products, row_bits)
    diagonal_terms = jnp.einsum(
        "srw,srv->swv",
        factor_rows.astype(jnp.float32),
        listed_products,
        precision=lax.Precision.HIGHEST,
    )
    diagonal_inverse = diag_inverse + lax.psum(diagonal_terms, ("row", "col"))
    row_total = lax.psum(listed_products, "col")
    column_inverse = -expand_pairs(row_total, row_bits)
    mirror_total = broadcast(row_total, "row", root_row)
    mirror_inverse = jnp.transpose(-expand_pairs(mirror_total, col_bits), (0, 2, 1))
    return (column_inverse, mirror_inverse, diagonal_inverse)


def solution(mesh):
    return jax.shard_map(
        local,
        mesh=mesh,
        in_specs=(P("row", "col"), P(None, "row", None), P(), P()),
        out_specs=(P(None, "row", None), P(None, None, "col"), P()),
        check_vma=False,
    )
```

profile of v0, /device:TPU:1, one launch (start us, length us, event | category | flops | bytes accessed | tf_op | source)
XLA Modules:
  0.0 641.8 jit_solution(4474671392308871341)
XLA Ops:
  8.0 0.8 broadcast_compare_fusion
  8.8 0.8 dynamic-slice_subtract_fusion
  9.6 49.3 %all-gather.2.cloned.1.call-done = bf16[2,6144,256]{2,1,0:T(8,128)(2,1)} async-done(((bf16[2,384,256]{2,1,0:T(8,128)(2,1)}), bf16[2,6144,256]{2,1,0:T(8,128)(2,1)}) %all-gather.2.cloned.1.call-update) | async-done | bytes 6291472 | tf_op jit(solution)/shard_map/all_gather | solution.py:59
  59.0 1.0 constant_dynamic-slice_fusion
  60.1 0.8 fusion.1
  61.9 1.5 convolution_bitcast_fusion
  64.4 1.2 fusion
  65.6 1.0 copy.11
  66.6 1.0 copy.10
  67.8 3.0 convolution_bitcast_fusion.2
  72.3 160.2 %all-reduce.4.cloned.1.call-done = f32[2,384,256]{2,1,0:T(8,128)} async-done(((f32[2,384,256]{2,1,0:T(8,128)}), f32[2,384,256]{2,1,0:T(8,128)}) %all-reduce.4.cloned.1.call-update) | async-done | bytes 786448 | tf_op jit(solution)/shard_map/psum | solution.py:72
  232.5 0.9 broadcast_select_fusion.1
  234.0 267.5 %all-reduce.8.cloned.1.call-done = f32[2,256,256]{1,2,0:T(8,128)} async-done(((f32[2,256,256]{1,2,0:T(8,128)}), f32[2,256,256]{1,2,0:T(8,128)}) %all-reduce.8.cloned.1.call-update) | async-done | bytes 524304 | tf_op jit(solution)/shard_map/psum | solution.py:71
  501.5 1.1 add.48
  502.6 1.0 copy.17
  504.0 1.7 broadcast_in_dim.104
  505.7 2.5 broadcast_in_dim.105
  508.2 1.3 select_negate_fusion
  509.5 3.0 copy.16
  512.5 115.7 %all-reduce.6.cloned.1.call-done = f32[2,3,128,256]{3,2,1,0:T(8,128)} async-done(((f32[2,3,128,256]{3,2,1,0:T(8,128)}), f32[2,3,128,256]{3,2,1,0:T(8,128)}) %all-reduce.6.cloned.1.call-update) | async-done | bytes 786448 | tf_op jit(solution)/shard_map/psum | solution.py:11
  628.2 1.5 copy.13
  629.8 1.7 broadcast_in_dim.112
  631.4 2.5 broadcast_in_dim.113
  634.0 1.3 negate_bitcast_fusion
  (35 shorter events, 5.4 us)
Async XLA Ops:
  7.2 53.8 %copy-start = (bf16[768,768]{1,0:T(8,128)(2,1)S(1)}, bf16[768,768]{1,0:T(8,128)(2,1)}, u32[]{:S(2)}) copy-start(bf16[768,768]{1,0:T(8,128)(2,1)} %param.4) | copy-start | bytes 3538948
  7.2 51.8 %all-gather.2.cloned.1.call-start = ((), (), s32[]{:S(2)}) async-start(), calls=%async_computation | async-start | bytes 6684672 | tf_op jit(solution)/shard_map/all_gather | solution.py:59
  67.8 3.0 copy-start.1
  70.8 161.8 %all-reduce.4.cloned.1.call-start = ((), (), s32[]{:S(2)}) async-start(), calls=%async_computation.1 | async-start | bytes 1572864 | tf_op jit(solution)/shard_map/psum | solution.py:72
  71.5 162.3 %copy-start.3 = (f32[2,256,256]{2,1,0:T(8,128)S(1)}, f32[2,256,256]{2,1,0:T(8,128)}, u32[]{:S(2)}) copy-start(f32[2,256,256]{2,1,0:T(8,128)} %param.7) | copy-start | bytes 1572868
  71.5 430.0 %all-reduce.8.cloned.1.call-start = ((), (), s32[]{:S(2)}) async-start(), calls=%async_computation.3 | async-start | bytes 1048576 | tf_op jit(solution)/shard_map/psum | solution.py:71
  72.2 556.0 %all-reduce.6.cloned.1.call-start = ((), (), s32[]{:S(2)}) async-start(), calls=%async_computation.2 | async-start | bytes 1572864 | tf_op jit(solution)/shard_map/psum | solution.py:11
  234.0 269.6 %copy-start.2 = (f32[2,384,256]{2,1,0:T(8,128)S(1)}, f32[2,384,256]{2,1,0:T(8,128)}, u32[]{:S(2)}) copy-start(f32[2,384,256]{2,1,0:T(8,128)} %all-reduce.4.cloned.1.call-done) | copy-start | bytes 2359300
Sparse Core Ops, SparseCore 0:
  9.8 49.1 all-gather.1
  74.8 157.7 all-reduce.3
  238.6 262.8 all-reduce.7
  504.0 124.2 all-reduce.5
where the time goes:
time: 642 us
  waiting for transfers between devices  595 us (93%)
  local copies, waits for them, and re-layouts  21.3 us (3%)
  between operations  14 us (2%)
  other arithmetic  6.57 us (1%)
    psum x1, waiting for transfers between devices, local(): diagonal_inverse = diag_inverse + lax.psum(diagonal_terms, ('row', 'col'))  268 us
    psum x1, waiting for transfers between devices, local(): row_total = lax.psum(listed_products, 'col')  160 us
    psum x1, waiting for transfers between devices, broadcast(): return lax.psum(jnp.where(mine, x, jnp.zeros_like(x)), axis)  116 us
    all_gather x1, waiting for transfers between devices, local(): gathered = lax.all_gather(factor_rows, 'row', axis=1, tiled=True)  49.3 us
  transfers between devices with their start and end apart: 4, of which 4 were waited for; matrix products, arithmetic and copies ran while one was open for 2% of the time, Pallas kernels for 0%

commit v1 on v0

v1 whole, which is shorter than its diff:
```python
import jax
import jax.numpy as jnp
from jax import lax
from jax.experimental import pallas as pl
from jax.experimental.pallas import tpu as pltpu
from jax.sharding import PartitionSpec as P

BS = 128
W = 256
CHIPS = 8
PIECE = 48
MESH = pl.DeviceIdType.MESH
F32 = jnp.float32
BF16 = jnp.bfloat16


def dot_t(a, b):
    return lax.dot_general(a, b, (((0,), (0,)), ((), ())), preferred_element_type=F32)


def comm_kernel(
    lists, a_hbm, f_hbm, diag, pc, pr, dout,
    a_v, f_v, asel, fp, pp, pcv, prv, half, rs, dp, dr, d1, dy, dz, dg,
    ld_sem, fs_send, fs_recv, on_send, on_recv, rs_send, rs_recv,
    ag_send, ag_recv, rl_send, rl_recv, tp_send, tp_recv, zs_send, zs_recv,
    ys_send, ys_recv, dr_send, dr_recv, dy_send, dy_recv, dz_send, dz_recv,
    dh_send, dh_recv, dg_send, dg_recv, do_send, do_recv,
):
    r = lax.axis_index("row")
    c = lax.axis_index("col")
    k = lax.rem(r, 2)
    j = r // 2
    y = lax.rem(c, 4)
    zh = c // 4
    mate = r + 1 - 2 * k
    ck = lax.rem(c, 2)
    cj = c // 2

    def chip(d):
        return lax.rem(j + d, CHIPS)

    def rcopy(src, dst, ssem, rsem, row, col):
        return pltpu.make_async_remote_copy(
            src_ref=src, dst_ref=dst, send_sem=ssem, recv_sem=rsem,
            device_id=(row, col), device_id_type=MESH,
        )

    barrier = pltpu.get_barrier_semaphore()

    @pl.when(r != c)
    def _():
        pl.semaphore_signal(barrier, inc=1, device_id=(c, r), device_id_type=MESH)

    for d in range(1, 4):
        zo = lax.rem(zh + d, 4)
        yo = lax.rem(y + d, 4)
        pl.semaphore_signal(barrier, inc=1, device_id=(r, zo * 4 + y), device_id_type=MESH)
        pl.semaphore_signal(barrier, inc=1, device_id=(r, zh * 4 + yo), device_id_type=MESH)

    def greet(d, carry):
        pl.semaphore_signal(barrier, inc=1, device_id=(lax.rem(r + d, 16), c), device_id_type=MESH)
        return carry

    lax.fori_loop(1, 16, greet, 0)

    load_a = pltpu.make_async_copy(a_hbm, a_v, ld_sem.at[0])
    load_f = pltpu.make_async_copy(f_hbm, f_v, ld_sem.at[1])
    load_a.start()
    load_f.start()
    load_a.wait()
    load_f.wait()

    def partial(s):
        for p in range(3):
            rb = lists[s, r * 3 + p] - 2 * (r * 3 + p)
            picked = jnp.where(
                rb == 0, a_v[p * 256 : p * 256 + 128, :], a_v[p * 256 + 128 : p * 256 + 256, :]
            )
            for q in range(3):
                cb = lists[s, c * 3 + q] - 2 * (c * 3 + q)
                asel[p * 128 : p * 128 + 128, q * 128 : q * 128 + 128] = jnp.where(
                    cb == 0, picked[:, q * 256 : q * 256 + 128], picked[:, q * 256 + 128 : q * 256 + 256]
                )
        got = dot_t(asel[...], f_v[s])
        pp[s] = got.reshape(CHIPS, PIECE, W)

    partial(1 - k)

    pl.semaphore_wait(barrier, jnp.where(r == c, 21, 22))

    swap = rcopy(pp.at[1 - k], half, on_send, on_recv, mate, c)
    swap.start()

    def fcopy(o):
        return rcopy(
            f_hbm.at[lax.rem(o, 2), pl.ds(pl.multiple_of((o // 2) * PIECE, PIECE), PIECE)],
            fp, fs_send.at[o], fs_recv, o, c,
        )

    @pl.when(r == c)
    def _():
        def scatter(d, carry):
            fcopy(lax.rem(r + d, 16)).start()
            return carry

        lax.fori_loop(1, 16, scatter, 0)
        fp[...] = f_v[k, pl.ds(pl.multiple_of(j * PIECE, PIECE), PIECE), :]

    partial(k)
    swap.wait_recv()

    pp[k] = pp[k] + half[...]

    def rs_copy(d, slot):
        o = chip(d)
        return rcopy(pp.at[k, o], rs.at[slot], rs_send.at[o], rs_recv.at[slot], 2 * o + k, c)

    def rs_start(d, carry):
        rs_copy(d, j).start()
        return carry

    lax.fori_loop(1, CHIPS, rs_start, 0)
    total = pp[k, j]
    for d in range(1, CHIPS):
        o = chip(CHIPS - d)
        rs_copy(d, o).wait_recv()
        total = total + rs[o]
    pcv[k, j] = total

    mine = k * CHIPS + j
    here = ck * CHIPS + cj
    cross = rcopy(pcv.at[k, j], prv.at[mine], tp_send, tp_recv, c, r)

    @pl.when(r != c)
    def _():
        cross.start()

    @pl.when(r == c)
    def _():
        prv[mine] = total

    def ag_copy(d, slot):
        return rcopy(pcv.at[k, slot], pcv.at[k, slot], ag_send.at[chip(d)], ag_recv.at[slot], 2 * chip(d) + k, c)

    def ag_start(d, carry):
        ag_copy(d, j).start()
        return carry

    lax.fori_loop(1, CHIPS, ag_start, 0)

    @pl.when(r != c)
    def _():
        fcopy(r).wait_recv()

    high = total.astype(BF16)
    low = (total - high.astype(F32)).astype(BF16)
    factor = fp[...]
    dp[...] = (dot_t(factor, high) + dot_t(factor, low)).reshape(CHIPS, 32, W)

    def dr_copy(d, slot):
        o = chip(d)
        return rcopy(dp.at[o], dr.at[slot], dr_send.at[o], dr_recv.at[slot], 2 * o + k, c)

    def dr_start(d, carry):
        dr_copy(d, j).start()
        return carry

    lax.fori_loop(1, CHIPS, dr_start, 0)

    def rl_copy(s, slot):
        return rcopy(pcv.at[s, slot], pcv.at[s, slot], rl_send.at[slot], rl_recv.at[slot], mate, c)

    rl_copy(k, j).start()

    def relay(d, carry):
        o = chip(CHIPS - d)
        ag_copy(d, o).wait_recv()
        rl_copy(k, o).start()
        return carry

    lax.fori_loop(1, CHIPS, relay, 0)

    dsum = dp[j]
    for d in range(1, CHIPS):
        o = chip(CHIPS - d)
        dr_copy(d, o).wait_recv()
        dsum = dsum + dr[o]
    d1[...] = dsum.reshape(4, 8, W)

    def line_y(d):
        return zh * 4 + lax.rem(y + d, 4)

    def line_z(d):
        return lax.rem(zh + d, 4) * 4 + y

    def dy_copy(d, slot):
        o = lax.rem(y + d, 4)
        return rcopy(d1.at[o], dy.at[slot], dy_send.at[o], dy_recv.at[slot], r, line_y(d))

    for d in range(1, 4):
        dy_copy(d, y).start()

    @pl.when(r != c)
    def _():
        rcopy(pcv.at[k, j], prv.at[here], tp_send, tp_recv, c, r).wait_recv()

    def slot_of(col):
        return lax.rem(col, 2) * CHIPS + col // 2

    def zs_copy(d, col):
        slot = slot_of(col)
        return rcopy(prv.at[slot], prv.at[slot], zs_send.at[lax.rem(zh + d, 4)], zs_recv.at[col // 4], r, line_z(d))

    for d in range(1, 4):
        zs_copy(d, c).start()

    def ys_copy(d, z, col):
        slot = slot_of(col)
        return rcopy(
            prv.at[slot], prv.at[slot], ys_send.at[z, lax.rem(y + d, 4)], ys_recv.at[z, lax.rem(col, 4)], r, line_y(d)
        )

    for d in range(1, 4):
        ys_copy(d, zh, c).start()

    dsum = d1[y]
    for d in range(1, 4):
        o = lax.rem(y + 4 - d, 4)
        dy_copy(d, o).wait_recv()
        dsum = dsum + dy[o]
    dz[zh] = dsum

    def dz_copy(d, slot):
        return rcopy(dz.at[slot], dz.at[slot], dz_send.at[lax.rem(zh + d, 4)], dz_recv.at[slot], r, line_z(d))

    for d in range(1, 4):
        dz_copy(d, zh).start()

    for d in range(1, 4):
        o = lax.rem(zh + 4 - d, 4)
        zs_copy(d, o * 4 + y).wait_recv()
        for e in range(1, 4):
            ys_copy(e, o, o * 4 + y).start()

    for d in range(1, 4):
        dz_copy(d, lax.rem(zh + 4 - d, 4)).wait_recv()
    dg[k, j, y] = (dz[0] + dz[1]) + (dz[2] + dz[3])

    def dh_copy(d, slot):
        return rcopy(
            dg.at[k, j, slot], dg.at[k, j, slot], dh_send.at[lax.rem(y + d, 4)], dh_recv.at[slot], r, line_y(d)
        )

    for d in range(1, 4):
        dh_copy(d, y).start()
    for d in range(1, 4):
        dh_copy(d, lax.rem(y + 4 - d, 4)).wait_recv()

    def dg_copy(d, slot):
        return rcopy(dg.at[k, slot], dg.at[k, slot], dg_send.at[chip(d)], dg_recv.at[slot], 2 * chip(d) + k, c)

    def dg_start(d, carry):
        dg_copy(d, j).start()
        return carry

    lax.fori_loop(1, CHIPS, dg_start, 0)

    for d in range(8):
        rl_copy(1 - k, d).wait_recv()
    pc[...] = pcv[...]
    for z in range(4):
        for d in range(1, 4):
            ys_copy(d, z, z * 4 + lax.rem(y + 4 - d, 4)).wait_recv()
    pr[...] = prv[...]

    def dg_wait(d, carry):
        dg_copy(d, chip(CHIPS - d)).wait_recv()
        return carry

    lax.fori_loop(1, CHIPS, dg_wait, 0)
    last = rcopy(dg.at[k], dg.at[k], do_send, do_recv, mate, c)
    last.start()
    rcopy(dg.at[1 - k], dg.at[1 - k], do_send, do_recv, mate, c).wait_recv()
    dout[...] = diag[...] + dg[...].reshape(2, W, W)

    last.wait_send()
    swap.wait_send()

    @pl.when(r != c)
    def _():
        cross.wait_send()

    @pl.when(r == c)
    def _():
        def scattered(d, carry):
            fcopy(lax.rem(r + d, 16)).wait_send()
            return carry

        lax.fori_loop(1, 16, scattered, 0)

    def drain(d, carry):
        rs_copy(d, j).wait_send()
        ag_copy(d, j).wait_send()
        dr_copy(d, j).wait_send()
        dg_copy(d, j).wait_send()
        return carry

    lax.fori_loop(1, CHIPS, drain, 0)
    for d in range(CHIPS):
        rl_copy(k, d).wait_send()
    for d in range(1, 4):
        dy_copy(d, y).wait_send()
        dz_copy(d, zh).wait_send()
        dh_copy(d, y).wait_send()
        zs_copy(d, c).wait_send()
        for z in range(4):
            ys_copy(d, z, z * 4 + y).wait_send()


def exchange(blocks_inverse, factor_rows, block_lists, diag_inverse):
    dma = pltpu.SemaphoreType.DMA
    vmem = pl.BlockSpec(memory_space=pltpu.VMEM)
    return pl.pallas_call(
        comm_kernel,
        out_shape=(
            jax.ShapeDtypeStruct((2, CHIPS, PIECE, W), F32),
            jax.ShapeDtypeStruct((16, PIECE, W), F32),
            jax.ShapeDtypeStruct((2, W, W), F32),
        ),
        in_specs=[
            pl.BlockSpec(memory_space=pltpu.SMEM),
            pl.BlockSpec(memory_space=pl.ANY),
            pl.BlockSpec(memory_space=pl.ANY),
            vmem,
        ],
        out_specs=(vmem, vmem, vmem),
        scratch_shapes=[
            pltpu.VMEM((768, 768), BF16),
            pltpu.VMEM((2, 384, W), BF16),
            pltpu.VMEM((384, 384), BF16),
            pltpu.VMEM((PIECE, W), BF16),
            pltpu.VMEM((2, CHIPS, PIECE, W), F32),
            pltpu.VMEM((2, CHIPS, PIECE, W), F32),
            pltpu.VMEM((16, PIECE, W), F32),
            pltpu.VMEM((CHIPS, PIECE, W), F32),
            pltpu.VMEM((CHIPS, PIECE, W), F32),
            pltpu.VMEM((CHIPS, 32, W), F32),
            pltpu.VMEM((CHIPS, 32, W), F32),
            pltpu.VMEM((4, 8, W), F32),
            pltpu.VMEM((4, 8, W), F32),
            pltpu.VMEM((4, 8, W), F32),
            pltpu.VMEM((2, CHIPS, 4, 8, W), F32),
            dma((2,)), dma((16,)), dma, dma, dma, dma((8,)), dma((8,)),
            dma((8,)), dma((8,)), dma((8,)), dma((8,)), dma, dma, dma((4,)), dma((4,)),
            dma((4, 4)), dma((4, 4)), dma((8,)), dma((8,)), dma((4,)), dma((4,)), dma((4,)), dma((4,)),
            dma((4,)), dma((4,)), dma((8,)), dma((8,)), dma, dma,
        ],
        compiler_params=pltpu.CompilerParams(collective_id=0, has_side_effects=True),
        name="exchange",
    )(block_lists, blocks_inverse, factor_rows, diag_inverse)


def expand(packed, bits):
    grouped = packed.reshape(2, 3, 1, BS, W)
    which = bits[:, :, None, None, None] == jnp.arange(2, dtype=jnp.int32)[None, None, :, None, None]
    return jnp.where(which, -grouped, 0.0).reshape(2, 768, W)


def pair_bits(block_lists, index):
    mine = lax.dynamic_slice_in_dim(block_lists, index * 3, 3, 1)
    return mine - 2 * (index * 3 + jnp.arange(3, dtype=jnp.int32))[None, :]


def local(blocks_inverse, factor_rows, block_lists, diag_inverse):
    col_packed, row_packed, diagonal = exchange(blocks_inverse, factor_rows, block_lists, diag_inverse)
    column = expand(row_packed, pair_bits(block_lists, lax.axis_index("row")))
    mirror = jnp.transpose(expand(col_packed, pair_bits(block_lists, lax.axis_index("col"))), (0, 2, 1))
    return column, mirror, diagonal


def solution(mesh):
    return jax.shard_map(
        local,
        mesh=mesh,
        in_specs=(P("row", "col"), P(None, "row", None), P(), P()),
        out_specs=(P(None, "row", None), P(None, None, "col"), P()),
        check_vma=False,
    )
```

time: 642 us -> 64.1 us (0.10)
  waiting for transfers between devices: 595 us -> 0 us
  Pallas kernels: 0 us -> 53.4 us
  local copies, waits for them, and re-layouts: 21.3 us -> 6.97 us
  between operations: 14 us -> 0.77 us
    psum x3 -> x0, waiting for transfers between devices: 543 us -> none  [the longest x1 268 us: local(): diagonal_inverse = diag_inverse + lax.psum(diagonal_terms, ('row', 'col'))]
    pallas_call x0 -> x1, Pallas kernels: none -> 53.4 us  [exchange(): pl.pallas_call(comm_kernel, out_shape=(jax.ShapeDtypeStruct((2, CHIPS, PI...]
    all_gather x1 -> x0, waiting for transfers between devices: 49.3 us -> none  [local(): gathered = lax.all_gather(factor_rows, 'row', axis=1, tiled=True)]
  transfers between devices with their start and end apart: 4 -> 0, of which waited for: 4 -> 0; matrix products, arithmetic and copies ran while one was open for 2% -> 0% of each run, Pallas kernels for 0% -> 0%
where the time goes in v1:
time: 64.1 us; the launch traced here: 63.9 us
  Pallas kernels  53.4 us (83%)
  local copies, waits for them, and re-layouts  6.97 us (11%)
  other arithmetic  2.8 us (4%)
  between operations  0.77 us (1%)
    pallas_call x1, Pallas kernels, exchange(): pl.pallas_call(comm_kernel, out_shape=(jax.ShapeDtypeStruct((2, CHIPS, PI...  53.4 us
    broadcast_in_dim x8, local copies, waits for them, and re-layouts, expand(): return jnp.where(which, -grouped, 0.0).reshape(2, 768, W)  3.8 us
    unnamed x8, local copies, waits for them, and re-layouts  2.42 us

profile of v1, /device:TPU:1, one launch (start us, length us, event | category | flops | bytes accessed | tf_op | source)
XLA Modules:
  0.0 63.9 jit_solution(9256812190835903729)
XLA Ops:
  0.6 53.4 %exchange.1 = (f32[2,8,48,256]{3,2,1,0:T(8,128)}, f32[16,48,256]{2,1,0:T(8,128)}, f32[2,256,256]{2,1,0:T(8,128)}) custom-call(s32[2,48]{1,0:T(2,128)} %lists.1, bf16[768,768]{1,0:T(8,128)(2,1)} %a_hbm.1, bf16[2,384,256]{2,1,0:T(8,128)(2,1)} %f_hbm.1, f32[2,256,256]{2,1,0:T(8,128)} %diag.1), custom_call_target="tpu_custom_call" | custom-call | tf_op jit(solution)/shard_map/exchange/pallas_call | solution.py:323
  54.0 1.2 %neg.22 = f32[16,48,256]{2,1,0:T(8,128)S(1)} negate(f32[16,48,256]{2,1,0:T(8,128)} %get-tuple-element.6) | non-fusion elementwise | flops 196608 | bytes 1572864 | tf_op jit(solution)/shard_map/neg | solution.py:366
  55.2 0.4 copy.10
  55.6 0.5 broadcast_in_dim.52
  56.1 0.0 copy-start.2
  56.2 1.3 %broadcast_in_dim.53 = f32[2,768,256]{1,2,0:T(8,128)S(1)} reshape(f32[2,3,2,128,256]{3,2,1,4,0:T(2,128)S(1)} %broadcast_in_dim.52) | data formatting | bytes 3145728 | tf_op jit(solution)/shard_map/jit(_where)/broadcast_in_dim | solution.py:366
  57.5 0.0 copy-done.2
  57.5 0.1 dynamic-slice_subtract_fusion
  57.5 0.1 iota_compare_fusion
  57.6 0.1 broadcast_in_dim.49
  57.7 0.1 broadcast_select_fusion
  57.8 0.0 copy-start
  57.9 1.6 %copy.12 = f32[2,768,256]{2,1,0:T(8,128)} copy(f32[2,768,256]{1,2,0:T(8,128)S(1)} %broadcast_select_fusion) | data formatting | bytes 3145728
  59.5 0.0 copy-done
  59.5 0.1 neg.24
  59.5 0.4 copy.11
  59.9 0.5 broadcast_in_dim.58
  60.5 1.3 %broadcast_in_dim.59 = f32[2,768,256]{1,2,0:T(8,128)S(1)} reshape(f32[2,3,2,128,256]{3,2,1,4,0:T(2,128)S(1)} %broadcast_in_dim.58) | data formatting | bytes 3145728 | tf_op jit(solution)/shard_map/jit(_where)/broadcast_in_dim | solution.py:366
  61.7 0.1 broadcast_in_dim.55
  61.8 0.0 copy-start.1
  61.8 1.3 %select_bitcast_fusion = f32[2,256,768]{2,1,0:T(8,128)} fusion(f32[2,768,256]{1,2,0:T(8,128)S(1)} %broadcast_in_dim.59, pred[2,768]{1,0:T(4,128)(4,1)S(1)} %broadcast_in_dim.56), kind=kLoop, calls=%fused_computation | loop fusion | flops 393216 | bytes 3147264 | tf_op jit(solution)/shard_map/transpose | solution.py:377
  63.1 0.0 copy-done.1
  63.1 0.8 %copy.14 = f32[2,256,256]{2,1,0:T(8,128)} copy(f32[2,256,256]{2,1,0:T(8,128)S(1)} %copy-done.1) | data formatting | bytes 1048576
  (4 shorter events, 0.1 us)
Async XLA Ops:
  56.1 1.3 %copy-start.2 = (s32[2,48]{1,0:T(2,128)S(1)}, s32[2,48]{1,0:T(2,128)}, u32[]{:S(2)}) copy-start(s32[2,48]{1,0:T(2,128)} %lists.1) | copy-start | bytes 1156
  57.8 1.6 %copy-start = (f32[2,8,48,256]{3,2,1,0:T(8,128)S(1)}, f32[2,8,48,256]{3,2,1,0:T(8,128)}, u32[]{:S(2)}) copy-start(f32[2,8,48,256]{3,2,1,0:T(8,128)} %get-tuple-element.7) | copy-start | bytes 2359300
  61.8 1.3 %copy-start.1 = (f32[2,256,256]{2,1,0:T(8,128)S(1)}, f32[2,256,256]{2,1,0:T(8,128)}, u32[]{:S(2)}) copy-start(f32[2,256,256]{2,1,0:T(8,128)} %get-tuple-element.24) | copy-start | bytes 1572868

commit v2 on v1

v2 whole, which is shorter than its diff:
```python
import jax
import jax.numpy as jnp
from jax import lax
from jax.experimental import pallas as pl
from jax.experimental.pallas import tpu as pltpu
from jax.sharding import PartitionSpec as P

BS = 128
W = 256
CHIPS = 8
PIECE = 48
MESH = pl.DeviceIdType.MESH
F32 = jnp.float32
BF16 = jnp.bfloat16


def dot_t(a, b):
    return lax.dot_general(a, b, (((0,), (0,)), ((), ())), preferred_element_type=F32)


def comm_kernel(
    lists, a_hbm, f_hbm, pc, pr, dout,
    a_v, f_v, asel, fp, pp, pcv, prv, half, rs, dp, dr, dz, dg,
    ld_sem, fs_send, fs_recv, on_send, on_recv, rs_send, rs_recv,
    ag_send, ag_recv, rl_send, rl_recv, tp_send, tp_recv, zs_send, zs_recv,
    ys_send, ys_recv, dr_send, dr_recv, dz_send, dz_recv,
    dg_send, dg_recv, do_send, do_recv, out_sem,
):
    r = lax.axis_index("row")
    c = lax.axis_index("col")
    k = lax.rem(r, 2)
    j = r // 2
    y = lax.rem(c, 4)
    zh = c // 4
    x = lax.rem(j, 4)
    zl = j // 4
    z = zh * 2 + zl
    q = x * 4 + y
    mate = r + 1 - 2 * k
    ck = lax.rem(c, 2)
    cj = c // 2

    def chip(d):
        return lax.rem(j + d, CHIPS)

    def rcopy(src, dst, ssem, rsem, row, col):
        return pltpu.make_async_remote_copy(
            src_ref=src, dst_ref=dst, send_sem=ssem, recv_sem=rsem,
            device_id=(row, col), device_id_type=MESH,
        )

    barrier = pltpu.get_barrier_semaphore()

    @pl.when(r != c)
    def _():
        pl.semaphore_signal(barrier, inc=1, device_id=(c, r), device_id_type=MESH)

    def greet_z(d, carry):
        zo = lax.rem(zh + d // 2, 4)
        pl.semaphore_signal(
            barrier, inc=1, device_id=(lax.rem(d, 2) * 8 + lax.rem(r, 8), zo * 4 + y), device_id_type=MESH
        )
        return carry

    lax.fori_loop(2, 8, greet_z, 0)

    def greet_y(d, carry):
        yo = lax.rem(y + d // 4, 4)
        pl.semaphore_signal(
            barrier, inc=1, device_id=(zl * 8 + lax.rem(d, 4) * 2 + k, zh * 4 + yo), device_id_type=MESH
        )
        return carry

    lax.fori_loop(4, 16, greet_y, 0)

    def greet(d, carry):
        pl.semaphore_signal(barrier, inc=1, device_id=(lax.rem(r + d, 16), c), device_id_type=MESH)
        return carry

    lax.fori_loop(1, 16, greet, 0)

    load_a = pltpu.make_async_copy(a_hbm, a_v, ld_sem.at[0])
    load_f = pltpu.make_async_copy(f_hbm, f_v, ld_sem.at[1])
    load_a.start()
    load_f.start()
    load_a.wait()
    load_f.wait()

    def partial(s):
        for p in range(3):
            rb = lists[s, r * 3 + p] - 2 * (r * 3 + p)
            picked = jnp.where(
                rb == 0, a_v[p * 256 : p * 256 + 128, :], a_v[p * 256 + 128 : p * 256 + 256, :]
            )
            for q in range(3):
                cb = lists[s, c * 3 + q] - 2 * (c * 3 + q)
                asel[p * 128 : p * 128 + 128, q * 128 : q * 128 + 128] = jnp.where(
                    cb == 0, picked[:, q * 256 : q * 256 + 128], picked[:, q * 256 + 128 : q * 256 + 256]
                )
        got = dot_t(asel[...], f_v[s])
        pp[s] = got.reshape(CHIPS, PIECE, W)

    partial(1 - k)

    pl.semaphore_wait(barrier, jnp.where(r == c, 33, 34))

    swap = rcopy(pp.at[1 - k], half, on_send, on_recv, mate, c)
    swap.start()

    def fcopy(o):
        return rcopy(
            f_hbm.at[lax.rem(o, 2), pl.ds(pl.multiple_of((o // 2) * PIECE, PIECE), PIECE)],
            fp, fs_send.at[o], fs_recv, o, c,
        )

    @pl.when(r == c)
    def _():
        def scatter(d, carry):
            fcopy(lax.rem(r + d, 16)).start()
            return carry

        lax.fori_loop(1, 16, scatter, 0)
        fp[...] = f_v[k, pl.ds(pl.multiple_of(j * PIECE, PIECE), PIECE), :]

    partial(k)
    swap.wait_recv()

    pp[k] = pp[k] + half[...]

    def rs_copy(d, slot):
        o = chip(d)
        return rcopy(pp.at[k, o], rs.at[slot], rs_send.at[o], rs_recv.at[slot], 2 * o + k, c)

    def rs_start(d, carry):
        rs_copy(d, j).start()
        return carry

    lax.fori_loop(1, CHIPS, rs_start, 0)
    total = pp[k, j]
    for d in range(1, CHIPS):
        o = chip(CHIPS - d)
        rs_copy(d, o).wait_recv()
        total = total + rs[o]
    pcv[k, j] = total

    mine = k * CHIPS + j
    here = ck * CHIPS + cj
    cross = rcopy(pcv.at[k, j], prv.at[mine], tp_send, tp_recv, c, r)

    @pl.when(r != c)
    def _():
        cross.start()

    @pl.when(r == c)
    def _():
        prv[mine] = total

    def ag_copy(d, slot):
        return rcopy(pcv.at[k, slot], pcv.at[k, slot], ag_send.at[chip(d)], ag_recv.at[slot], 2 * chip(d) + k, c)

    def ag_start(d, carry):
        ag_copy(d, j).start()
        return carry

    lax.fori_loop(1, CHIPS, ag_start, 0)

    @pl.when(r != c)
    def _():
        fcopy(r).wait_recv()

    high = total.astype(BF16)
    low = (total - high.astype(F32)).astype(BF16)
    left = fp[:, :128]
    right = fp[:, 128:]
    top = dot_t(left, high) + dot_t(left, low)
    dp[0:128, :] = top[:, :128]
    dp[128:256, :] = top[:, 128:]
    dp[256:384, :] = dot_t(right, high[:, 128:]) + dot_t(right, low[:, 128:])

    def around(d):
        return lax.rem(q + d, 16)

    def rows24(o):
        return pl.ds(pl.multiple_of(o * 24, 8), 24)

    def dr_copy(d, slot):
        o = around(d)
        return rcopy(
            dp.at[rows24(o)], dr.at[slot], dr_send.at[o], dr_recv.at[slot],
            zl * 8 + (o // 4) * 2 + k, zh * 4 + lax.rem(o, 4),
        )

    def dr_start(d, carry):
        dr_copy(d, q).start()
        return carry

    lax.fori_loop(1, 16, dr_start, 0)

    def rl_copy(s, slot):
        return rcopy(pcv.at[s, slot], pcv.at[s, slot], rl_send.at[slot], rl_recv.at[slot], mate, c)

    rl_copy(k, j).start()

    def relay(d, carry):
        o = chip(CHIPS - d)
        ag_copy(d, o).wait_recv()
        rl_copy(k, o).start()
        return carry

    lax.fori_loop(1, CHIPS, relay, 0)

    def dr_add(d, acc):
        o = around(16 - d)
        dr_copy(d, o).wait_recv()
        return acc + dr[o]

    dz[z] = lax.fori_loop(1, 16, dr_add, dp[rows24(q), :])

    def dz_copy(d, slot):
        o = lax.rem(z + d, 8)
        return rcopy(
            dz.at[slot], dz.at[slot], dz_send.at[o], dz_recv.at[slot],
            lax.rem(o, 2) * 8 + lax.rem(r, 8), (o // 2) * 4 + y,
        )

    def dz_start(d, carry):
        dz_copy(d, z).start()
        return carry

    lax.fori_loop(1, 8, dz_start, 0)

    def line_y(d):
        return zh * 4 + lax.rem(y + d, 4)

    def line_z(d):
        return lax.rem(zh + d, 4) * 4 + y

    @pl.when(r != c)
    def _():
        rcopy(pcv.at[k, j], prv.at[here], tp_send, tp_recv, c, r).wait_recv()

    def slot_of(col):
        return lax.rem(col, 2) * CHIPS + col // 2

    def zs_copy(d, col):
        slot = slot_of(col)
        return rcopy(prv.at[slot], prv.at[slot], zs_send.at[lax.rem(zh + d, 4)], zs_recv.at[col // 4], r, line_z(d))

    for d in range(1, 4):
        zs_copy(d, c).start()

    def ys_copy(d, w, col):
        slot = slot_of(col)
        return rcopy(
            prv.at[slot], prv.at[slot], ys_send.at[w, lax.rem(y + d, 4)], ys_recv.at[w, lax.rem(col, 4)], r, line_y(d)
        )

    for d in range(1, 4):
        ys_copy(d, zh, c).start()

    for d in range(1, 4):
        o = lax.rem(zh + 4 - d, 4)
        zs_copy(d, o * 4 + y).wait_recv()
        for e in range(1, 4):
            ys_copy(e, o, o * 4 + y).start()

    def dz_wait(d, carry):
        dz_copy(d, lax.rem(z + 8 - d, 8)).wait_recv()
        return carry

    lax.fori_loop(1, 8, dz_wait, 0)
    dg[k, rows24(q), :] = ((dz[0] + dz[1]) + (dz[2] + dz[3])) + ((dz[4] + dz[5]) + (dz[6] + dz[7]))

    def dg_copy(d, slot):
        o = around(d)
        return rcopy(
            dg.at[k, rows24(slot)], dg.at[k, rows24(slot)], dg_send.at[o], dg_recv.at[slot],
            zl * 8 + (o // 4) * 2 + k, zh * 4 + lax.rem(o, 4),
        )

    def do_copy(s, slot):
        return rcopy(dg.at[s, rows24(slot)], dg.at[s, rows24(slot)], do_send.at[slot], do_recv.at[slot], mate, c)

    def dg_start(d, carry):
        dg_copy(d, q).start()
        return carry

    lax.fori_loop(1, 16, dg_start, 0)
    do_copy(k, q).start()

    for d in range(8):
        rl_copy(1 - k, d).wait_recv()
    out_pc = pltpu.make_async_copy(pcv, pc, out_sem.at[0])
    out_pc.start()
    for w in range(4):
        for d in range(1, 4):
            ys_copy(d, w, w * 4 + lax.rem(y + 4 - d, 4)).wait_recv()
    out_pr = pltpu.make_async_copy(prv, pr, out_sem.at[1])
    out_pr.start()

    def dg_relay(d, carry):
        o = around(16 - d)
        dg_copy(d, o).wait_recv()
        do_copy(k, o).start()
        return carry

    lax.fori_loop(1, 16, dg_relay, 0)

    def do_wait(d, carry):
        do_copy(1 - k, d).wait_recv()
        return carry

    lax.fori_loop(0, 16, do_wait, 0)
    out_d = pltpu.make_async_copy(dg, dout, out_sem.at[2])
    out_d.start()

    swap.wait_send()

    @pl.when(r != c)
    def _():
        cross.wait_send()

    @pl.when(r == c)
    def _():
        def scattered(d, carry):
            fcopy(lax.rem(r + d, 16)).wait_send()
            return carry

        lax.fori_loop(1, 16, scattered, 0)

    def drain(d, carry):
        rs_copy(d, j).wait_send()
        ag_copy(d, j).wait_send()
        dz_copy(d, z).wait_send()
        return carry

    lax.fori_loop(1, CHIPS, drain, 0)
    for d in range(CHIPS):
        rl_copy(k, d).wait_send()
    for d in range(1, 4):
        zs_copy(d, c).wait_send()
        for w in range(4):
            ys_copy(d, w, w * 4 + y).wait_send()

    def drain_plane(d, carry):
        dr_copy(d, q).wait_send()
        dg_copy(d, q).wait_send()
        return carry

    lax.fori_loop(1, 16, drain_plane, 0)

    def drain_relay(d, carry):
        do_copy(k, d).wait_send()
        return carry

    lax.fori_loop(0, 16, drain_relay, 0)
    out_pc.wait()
    out_pr.wait()
    out_d.wait()


def exchange(blocks_inverse, factor_rows, block_lists):
    dma = pltpu.SemaphoreType.DMA
    hbm = pl.BlockSpec(memory_space=pl.ANY)
    return pl.pallas_call(
        comm_kernel,
        out_shape=(
            jax.ShapeDtypeStruct((2, CHIPS, PIECE, W), F32),
            jax.ShapeDtypeStruct((16, PIECE, W), F32),
            jax.ShapeDtypeStruct((2, 384, 128), F32),
        ),
        in_specs=[pl.BlockSpec(memory_space=pltpu.SMEM), hbm, hbm],
        out_specs=(hbm, hbm, hbm),
        scratch_shapes=[
            pltpu.VMEM((768, 768), BF16),
            pltpu.VMEM((2, 384, W), BF16),
            pltpu.VMEM((384, 384), BF16),
            pltpu.VMEM((PIECE, W), BF16),
            pltpu.VMEM((2, CHIPS, PIECE, W), F32),
            pltpu.VMEM((2, CHIPS, PIECE, W), F32),
            pltpu.VMEM((16, PIECE, W), F32),
            pltpu.VMEM((CHIPS, PIECE, W), F32),
            pltpu.VMEM((CHIPS, PIECE, W), F32),
            pltpu.VMEM((384, 128), F32),
            pltpu.VMEM((16, 24, 128), F32),
            pltpu.VMEM((8, 24, 128), F32),
            pltpu.VMEM((2, 384, 128), F32),
            dma((2,)), dma((16,)), dma, dma, dma, dma((8,)), dma((8,)),
            dma((8,)), dma((8,)), dma((8,)), dma((8,)), dma, dma, dma((4,)), dma((4,)),
            dma((4, 4)), dma((4, 4)), dma((16,)), dma((16,)), dma((8,)), dma((8,)),
            dma((16,)), dma((16,)), dma((16,)), dma((16,)), dma((3,)),
        ],
        compiler_params=pltpu.CompilerParams(collective_id=0, has_side_effects=True),
        name="exchange",
    )(block_lists, blocks_inverse, factor_rows)


def expand_kernel(lists, pc, pr, dg, diag, column, mirror, diagonal, col_in, row_in, dg_in, diag_in, row_out, col_out, zero, d_out, in_sem, z_sem, o_sem):
    r = lax.axis_index("row")
    c = lax.axis_index("col")
    loads = [
        pltpu.make_async_copy(pr, row_in, in_sem.at[0]),
        pltpu.make_async_copy(pc, col_in, in_sem.at[1]),
        pltpu.make_async_copy(dg, dg_in, in_sem.at[2]),
        pltpu.make_async_copy(diag, diag_in, in_sem.at[3]),
    ]
    for load in loads:
        load.start()
    zero[...] = jnp.zeros_like(zero)
    stores = []

    def put(src, dst, sem):
        copy = pltpu.make_async_copy(src, dst, sem)
        copy.start()
        stores.append(copy)

    def span(block):
        return pl.ds(pl.multiple_of(block * BS, BS), BS)

    row_at = {}
    col_at = {}
    for s in range(2):
        for p in range(3):
            row_at[s, p] = lists[s, r * 3 + p] - 2 * (r * 3 + p)
            col_at[s, p] = lists[s, c * 3 + p] - 2 * (c * 3 + p)
            put(zero.at[0:128, :], column.at[s, span(2 * p + 1 - row_at[s, p])], z_sem.at[0, s, p])
            put(zero.at[:, 0:128], mirror.at[s, :, span(2 * p + 1 - col_at[s, p])], z_sem.at[1, s, p])
    loads[0].wait()
    for s in range(2):
        for p in range(3):
            row_out[s, p] = -row_in[s, p * BS : p * BS + BS, :]
            put(row_out.at[s, p], column.at[s, span(2 * p + row_at[s, p])], o_sem.at[0, s, p])
    loads[1].wait()
    for s in range(2):
        for p in range(3):
            col_out[s, p] = -jnp.transpose(col_in[s, p * BS : p * BS + BS, :])
            put(col_out.at[s, p], mirror.at[s, :, span(2 * p + col_at[s, p])], o_sem.at[1, s, p])
    loads[2].wait()
    loads[3].wait()
    for s in range(2):
        upper = dg_in[s, 128:256, :]
        d_out[s, 0:128, 0:128] = diag_in[s, 0:128, 0:128] + dg_in[s, 0:128, :]
        d_out[s, 0:128, 128:256] = diag_in[s, 0:128, 128:256] + upper
        d_out[s, 128:256, 0:128] = diag_in[s, 128:256, 0:128] + jnp.transpose(upper)
        d_out[s, 128:256, 128:256] = diag_in[s, 128:256, 128:256] + dg_in[s, 256:384, :]
    put(d_out, diagonal, in_sem.at[4])
    for store in stores:
        store.wait()


def expand(block_lists, col_packed, row_packed, upper, diag_inverse):
    dma = pltpu.SemaphoreType.DMA
    hbm = pl.BlockSpec(memory_space=pl.ANY)
    return pl.pallas_call(
        expand_kernel,
        out_shape=(
            jax.ShapeDtypeStruct((2, 768, W), F32),
            jax.ShapeDtypeStruct((2, W, 768), F32),
            jax.ShapeDtypeStruct((2, W, W), F32),
        ),
        in_specs=[pl.BlockSpec(memory_space=pltpu.SMEM)] + [hbm] * 4,
        out_specs=(hbm, hbm, hbm),
        scratch_shapes=[
            pltpu.VMEM((2, 384, W), F32),
            pltpu.VMEM((2, 384, W), F32),
            pltpu.VMEM((2, 384, 128), F32),
            pltpu.VMEM((2, W, W), F32),
            pltpu.VMEM((2, 3, BS, W), F32),
            pltpu.VMEM((2, 3, W, BS), F32),
            pltpu.VMEM((W, W), F32),
            pltpu.VMEM((2, W, W), F32),
            dma((5,)), dma((2, 2, 3)), dma((2, 2, 3)),
        ],
        name="expand",
    )(block_lists, col_packed, row_packed, upper, diag_inverse)


def local(blocks_inverse, factor_rows, block_lists, diag_inverse):
    col_packed, row_packed, upper = exchange(blocks_inverse, factor_rows, block_lists)
    return expand(
        block_lists, col_packed.reshape(2, 384, W), row_packed.reshape(2, 384, W), upper, diag_inverse
    )


def solution(mesh):
    return jax.shard_map(
        local,
        mesh=mesh,
        in_specs=(P("row", "col"), P(None, "row", None), P(), P()),
        out_specs=(P(None, "row", None), P(None, None, "col"), P()),
        check_vma=False,
    )
```

time: 64.1 us -> 59.8 us (0.933)
  local copies, waits for them, and re-layouts: 6.97 us -> 0 us
  Pallas kernels: 53.4 us -> 58.9 us
  other arithmetic: 2.8 us -> 0 us
    pallas_call x0 -> x1, Pallas kernels: none -> 4.08 us  [expand(): pl.pallas_call(expand_kernel, out_shape=(jax.ShapeDtypeStruct((2, 768, W)...]
    broadcast_in_dim x8 -> x0, local copies, waits for them, and re-layouts: 3.8 us -> none  [expand(): return jnp.where(which, -grouped, 0.0).reshape(2, 768, W)]
    unnamed x8 -> x0, local copies, waits for them, and re-layouts: 2.42 us -> none
    pallas_call x1, Pallas kernels: 53.4 us -> 54.8 us  [exchange(): pl.pallas_call(comm_kernel, out_shape=(jax.ShapeDtypeStruct((2, CHIPS, PI...]
    transpose x1 -> x0, other arithmetic: 1.27 us -> none  [local(): jnp.transpose(expand(col_packed, pair_bits(block_lists, lax.axis_index('c...]
    neg x2 -> x0, other arithmetic: 1.25 us -> none  [expand(): return jnp.where(which, -grouped, 0.0).reshape(2, 768, W)]
    neg x2 -> x0, local copies, waits for them, and re-layouts: 0.75 us -> none  [expand(): return jnp.where(which, -grouped, 0.0).reshape(2, 768, W)]
where the time goes in v2:
time: 59.8 us; the launch traced here: 59.6 us
  Pallas kernels  58.9 us (98%)
  between operations  0.64 us (1%)
    pallas_call x1, Pallas kernels, exchange(): pl.pallas_call(comm_kernel, out_shape=(jax.ShapeDtypeStruct((2, CHIPS, PI...  54.8 us
    pallas_call x1, Pallas kernels, expand(): pl.pallas_call(expand_kernel, out_shape=(jax.ShapeDtypeStruct((2, 768, W)...  4.08 us

profile of v2, /device:TPU:1, one launch (start us, length us, event | category | flops | bytes accessed | tf_op | source)
XLA Modules:
  0.0 59.6 jit_solution(489463018271814516)
XLA Ops:
  0.6 54.8 %exchange.1 = (f32[2,8,48,256]{3,2,1,0:T(8,128)}, f32[16,48,256]{2,1,0:T(8,128)}, f32[2,384,128]{2,1,0:T(8,128)}) custom-call(s32[2,48]{1,0:T(2,128)} %lists.3, bf16[768,768]{1,0:T(8,128)(2,1)} %a_hbm.1, bf16[2,384,256]{2,1,0:T(8,128)(2,1)} %f_hbm.1), custom_call_target="tpu_custom_call" | custom-call | tf_op jit(solution)/shard_map/exchange/pallas_call | solution.py:365
  55.5 4.1 %expand.1 = (f32[2,768,256]{2,1,0:T(8,128)}, f32[2,256,768]{2,1,0:T(8,128)}, f32[2,256,256]{2,1,0:T(8,128)}) custom-call(s32[2,48]{1,0:T(2,128)} %lists.3, f32[2,384,256]{2,1,0:T(8,128)} %bitcast.2, f32[2,384,256]{2,1,0:T(8,128)} %bitcast.3, f32[2,384,128]{2,1,0:T(8,128)} %get-tuple-element.8.dg, f32[2,256,256]{2,1,0:T(8,128)} %diag.1), custom_call_target="tpu_custom_call" | custom-call | tf_op jit(solution)/shard_map/expand/pallas_call | solution.py:454

commit v3 on v2

--- a/solution.py
+++ b/solution.py
@@ -9,6 +9,8 @@
 W = 256
 CHIPS = 8
 PIECE = 48
+CODED = 112
+TOP = 32000.0
 MESH = pl.DeviceIdType.MESH
 F32 = jnp.float32
 BF16 = jnp.bfloat16
@@ -18,9 +20,29 @@
     return lax.dot_general(a, b, (((0,), (0,)), ((), ())), preferred_element_type=F32)
 
 
+def encode(piece):
+    parts = []
+    steps = []
+    for half in range(2):
+        part = piece[:, half * 128 : half * 128 + 128]
+        most = jnp.max(jnp.abs(part), axis=0, keepdims=True)
+        level = jnp.clip(jnp.ceil(8.0 * jnp.log2(jnp.maximum(most, 1e-30))), -800.0, 1000.0)
+        factor = jnp.exp2(level * -0.125) * TOP
+        parts.append(jnp.round(part * factor).astype(jnp.int32).astype(jnp.int16))
+        steps.append(jnp.broadcast_to(level, (8, 128)))
+    steps = jnp.concatenate(steps, axis=0).astype(jnp.int32).astype(jnp.int16)
+    return jnp.concatenate(parts + [steps], axis=0)
+
+
+def decode_half(coded, half):
+    level = coded[96:112, :].astype(jnp.int32).astype(F32)[8 * half : 8 * half + 1, :]
+    step = jnp.exp2(level * 0.125) * (-1.0 / TOP)
+    return coded[PIECE * half : PIECE * half + PIECE, :].astype(jnp.int32).astype(F32) * step
+
+
 def comm_kernel(
     lists, a_hbm, f_hbm, pc, pr, dout,
-    a_v, f_v, asel, fp, pp, pcv, prv, half, rs, dp, dr, dz, dg,
+    a_v, f_v, asel, fp, pp, pcv, prv, half, rs, dp, dr, dz, dg, pcf, prf, pct,
     ld_sem, fs_send, fs_recv, on_send, on_recv, rs_send, rs_recv,
     ag_send, ag_recv, rl_send, rl_recv, tp_send, tp_recv, zs_send, zs_recv,
     ys_send, ys_recv, dr_send, dr_recv, dz_send, dz_recv,
@@ -141,29 +163,6 @@
         o = chip(CHIPS - d)
         rs_copy(d, o).wait_recv()
         total = total + rs[o]
-    pcv[k, j] = total
-
-    mine = k * CHIPS + j
-    here = ck * CHIPS + cj
-    cross = rcopy(pcv.at[k, j], prv.at[mine], tp_send, tp_recv, c, r)
-
-    @pl.when(r != c)
-    def _():
-        cross.start()
-
-    @pl.when(r == c)
-    def _():
-        prv[mine] = total
-
-    def ag_copy(d, slot):
-        return rcopy(pcv.at[k, slot], pcv.at[k, slot], ag_send.at[chip(d)], ag_recv.at[slot], 2 * chip(d) + k, c)
-
-    def ag_start(d, carry):
-        ag_copy(d, j).start()
-        return carry
-
-    lax.fori_loop(1, CHIPS, ag_start, 0)
-
     @pl.when(r != c)
     def _():
         fcopy(r).wait_recv()
@@ -196,6 +195,29 @@
 
     lax.fori_loop(1, 16, dr_start, 0)
 
+    pcv[k, j] = encode(total)
+
+    mine = k * CHIPS + j
+    here = ck * CHIPS + cj
+    cross = rcopy(pcv.at[k, j], prv.at[mine], tp_send, tp_recv, c, r)
+
+    @pl.when(r != c)
+    def _():
+        cross.start()
+
+    @pl.when(r == c)
+    def _():
+        prv[mine] = encode(total)
+
+    def ag_copy(d, slot):
+        return rcopy(pcv.at[k, slot], pcv.at[k, slot], ag_send.at[chip(d)], ag_recv.at[slot], 2 * chip(d) + k, c)
+
+    def ag_start(d, carry):
+        ag_copy(d, j).start()
+        return carry
+
+    lax.fori_loop(1, CHIPS, ag_start, 0)
+
     def rl_copy(s, slot):
         return rcopy(pcv.at[s, slot], pcv.at[s, slot], rl_send.at[slot], rl_recv.at[slot], mate, c)
 
@@ -290,12 +312,33 @@
 
     for d in range(8):
         rl_copy(1 - k, d).wait_recv()
-    out_pc = pltpu.make_async_copy(pcv, pc, out_sem.at[0])
+
+    def open_pc(o, carry):
+        rows = pl.ds(pl.multiple_of(lax.rem(o, 8) * PIECE, 8), PIECE)
+        coded = pcv[o // 8, lax.rem(o, 8)]
+        pcf[o // 8, rows, 0:128] = decode_half(coded, 0)
+        pcf[o // 8, rows, 128:256] = decode_half(coded, 1)
+        return carry
+
+    lax.fori_loop(0, 16, open_pc, 0)
+    for s in range(2):
+        for p in range(3):
+            pct[s, :, p * BS : p * BS + BS] = jnp.transpose(pcf[s, p * BS : p * BS + BS, :])
+    out_pc = pltpu.make_async_copy(pct, pc, out_sem.at[0])
     out_pc.start()
     for w in range(4):
         for d in range(1, 4):
             ys_copy(d, w, w * 4 + lax.rem(y + 4 - d, 4)).wait_recv()
-    out_pr = pltpu.make_async_copy(prv, pr, out_sem.at[1])
+
+    def open_pr(o, carry):
+        rows = pl.ds(pl.multiple_of(lax.rem(o, 8) * PIECE, 8), PIECE)
+        coded = prv[o]
+        prf[o // 8, rows, 0:128] = decode_half(coded, 0)
+        prf[o // 8, rows, 128:256] = decode_half(coded, 1)
+        return carry
+
+    lax.fori_loop(0, 16, open_pr, 0)
+    out_pr = pltpu.make_async_copy(prf, pr, out_sem.at[1])
     out_pr.start()
 
     def dg_relay(d, carry):
@@ -365,8 +408,8 @@
     return pl.pallas_call(
         comm_kernel,
         out_shape=(
-            jax.ShapeDtypeStruct((2, CHIPS, PIECE, W), F32),
-            jax.ShapeDtypeStruct((16, PIECE, W), F32),
+            jax.ShapeDtypeStruct((2, W, 384), F32),
+            jax.ShapeDtypeStruct((2, 384, W), F32),
             jax.ShapeDtypeStruct((2, 384, 128), F32),
         ),
         in_specs=[pl.BlockSpec(memory_space=pltpu.SMEM), hbm, hbm],
@@ -377,14 +420,17 @@
             pltpu.VMEM((384, 384), BF16),
             pltpu.VMEM((PIECE, W), BF16),
             pltpu.VMEM((2, CHIPS, PIECE, W), F32),
-            pltpu.VMEM((2, CHIPS, PIECE, W), F32),
-            pltpu.VMEM((16, PIECE, W), F32),
+            pltpu.VMEM((2, CHIPS, CODED, 128), jnp.int16),
+            pltpu.VMEM((16, CODED, 128), jnp.int16),
             pltpu.VMEM((CHIPS, PIECE, W), F32),
             pltpu.VMEM((CHIPS, PIECE, W), F32),
             pltpu.VMEM((384, 128), F32),
             pltpu.VMEM((16, 24, 128), F32),
             pltpu.VMEM((8, 24, 128), F32),
             pltpu.VMEM((2, 384, 128), F32),
+            pltpu.VMEM((2, 384, W), F32),
+            pltpu.VMEM((2, 384, W), F32),
+            pltpu.VMEM((2, W, 384), F32),
             dma((2,)), dma((16,)), dma, dma, dma, dma((8,)), dma((8,)),
             dma((8,)), dma((8,)), dma((8,)), dma((8,)), dma, dma, dma((4,)), dma((4,)),
             dma((4, 4)), dma((4, 4)), dma((16,)), dma((16,)), dma((8,)), dma((8,)),
@@ -395,55 +441,52 @@
     )(block_lists, blocks_inverse, factor_rows)
 
 
-def expand_kernel(lists, pc, pr, dg, diag, column, mirror, diagonal, col_in, row_in, dg_in, diag_in, row_out, col_out, zero, d_out, in_sem, z_sem, o_sem):
+def expand_kernel(
+    lists, pc, pr, dg, diag, column, mirror, diagonal, col_in, row_in, dg_in, diag_in, zero, d_out,
+    r_sem, c_sem, d_sem, z_sem, o_sem,
+):
     r = lax.axis_index("row")
     c = lax.axis_index("col")
-    loads = [
-        pltpu.make_async_copy(pr, row_in, in_sem.at[0]),
-        pltpu.make_async_copy(pc, col_in, in_sem.at[1]),
-        pltpu.make_async_copy(dg, dg_in, in_sem.at[2]),
-        pltpu.make_async_copy(diag, diag_in, in_sem.at[3]),
-    ]
-    for load in loads:
-        load.start()
-    zero[...] = jnp.zeros_like(zero)
     stores = []
 
-    def put(src, dst, sem):
+    def begin(src, dst, sem):
         copy = pltpu.make_async_copy(src, dst, sem)
         copy.start()
-        stores.append(copy)
+        return copy
 
     def span(block):
         return pl.ds(pl.multiple_of(block * BS, BS), BS)
 
+    loads_d = [begin(dg, dg_in, d_sem.at[0]), begin(diag, diag_in, d_sem.at[1])]
+    loads = {}
+    for s in range(2):
+        for p in range(3):
+            loads[0, s, p] = begin(pr.at[s, p * BS : p * BS + BS, :], row_in.at[s, p], r_sem.at[s, p])
+            loads[1, s, p] = begin(pc.at[s, :, p * BS : p * BS + BS], col_in.at[s, p], c_sem.at[s, p])
+    zero[...] = jnp.zeros_like(zero)
     row_at = {}
     col_at = {}
     for s in range(2):
         for p in range(3):
             row_at[s, p] = lists[s, r * 3 + p] - 2 * (r * 3 + p)
             col_at[s, p] = lists[s, c * 3 + p] - 2 * (c * 3 + p)
-            put(zero.at[0:128, :], column.at[s, span(2 * p + 1 - row_at[s, p])], z_sem.at[0, s, p])
-            put(zero.at[:, 0:128], mirror.at[s, :, span(2 * p + 1 - col_at[s, p])], z_sem.at[1, s, p])
-    loads[0].wait()
-    for s in range(2):
-        for p in range(3):
-            row_out[s, p] = -row_in[s, p * BS : p * BS + BS, :]
-            put(row_out.at[s, p], column.at[s, span(2 * p + row_at[s, p])], o_sem.at[0, s, p])
-    loads[1].wait()
-    for s in range(2):
-        for p in range(3):
-            col_out[s, p] = -jnp.transpose(col_in[s, p * BS : p * BS + BS, :])
-            put(col_out.at[s, p], mirror.at[s, :, span(2 * p + col_at[s, p])], o_sem.at[1, s, p])
-    loads[2].wait()
-    loads[3].wait()
+            stores.append(begin(zero.at[0:128, :], column.at[s, span(2 * p + 1 - row_at[s, p])], z_sem.at[0, s, p]))
+            stores.append(begin(zero.at[:, 0:128], mirror.at[s, :, span(2 * p + 1 - col_at[s, p])], z_sem.at[1, s, p]))
+    for load in loads_d:
+        load.wait()
     for s in range(2):
         upper = dg_in[s, 128:256, :]
         d_out[s, 0:128, 0:128] = diag_in[s, 0:128, 0:128] + dg_in[s, 0:128, :]
         d_out[s, 0:128, 128:256] = diag_in[s, 0:128, 128:256] + upper
         d_out[s, 128:256, 0:128] = diag_in[s, 128:256, 0:128] + jnp.transpose(upper)
         d_out[s, 128:256, 128:256] = diag_in[s, 128:256, 128:256] + dg_in[s, 256:384, :]
-    put(d_out, diagonal, in_sem.at[4])
+    stores.append(begin(d_out, diagonal, d_sem.at[2]))
+    for s in range(2):
+        for p in range(3):
+            loads[0, s, p].wait()
+            stores.append(begin(row_in.at[s, p], column.at[s, span(2 * p + row_at[s, p])], o_sem.at[0, s, p]))
+            loads[1, s, p].wait()
+            stores.append(begin(col_in.at[s, p], mirror.at[s, :, span(2 * p + col_at[s, p])], o_sem.at[1, s, p]))
     for store in stores:
         store.wait()
 
@@ -461,15 +504,13 @@
         in_specs=[pl.BlockSpec(memory_space=pltpu.SMEM)] + [hbm] * 4,
         out_specs=(hbm, hbm, hbm),
         scratch_shapes=[
-            pltpu.VMEM((2, 384, W), F32),
-            pltpu.VMEM((2, 384, W), F32),
+            pltpu.VMEM((2, 3, W, BS), F32),
+            pltpu.VMEM((2, 3, BS, W), F32),
             pltpu.VMEM((2, 384, 128), F32),
             pltpu.VMEM((2, W, W), F32),
-            pltpu.VMEM((2, 3, BS, W), F32),
-            pltpu.VMEM((2, 3, W, BS), F32),
             pltpu.VMEM((W, W), F32),
             pltpu.VMEM((2, W, W), F32),
-            dma((5,)), dma((2, 2, 3)), dma((2, 2, 3)),
+            dma((2, 3)), dma((2, 3)), dma((3,)), dma((2, 2, 3)), dma((2, 2, 3)),
         ],
         name="expand",
     )(block_lists, col_packed, row_packed, upper, diag_inverse)
@@ -478,7 +519,7 @@
 def local(blocks_inverse, factor_rows, block_lists, diag_inverse):
     col_packed, row_packed, upper = exchange(blocks_inverse, factor_rows, block_lists)
     return expand(
-        block_lists, col_packed.reshape(2, 384, W), row_packed.reshape(2, 384, W), upper, diag_inverse
+        block_lists, col_packed, row_packed, upper, diag_inverse
     )
 
 

time: 59.8 us -> 53.6 us (0.90)
  Pallas kernels: 58.9 us -> 52.8 us
    pallas_call x1, Pallas kernels: 54.8 us -> 48 us  [exchange(): pl.pallas_call(comm_kernel, out_shape=(jax.ShapeDtypeStruct((2, W, 384),...]
    pallas_call x1, Pallas kernels: 4.08 us -> 4.73 us  [expand(): pl.pallas_call(expand_kernel, out_shape=(jax.ShapeDtypeStruct((2, 768, W)...]
where the time goes in v3:
time: 53.6 us; the launch traced here: 53.4 us
  Pallas kernels  52.8 us (99%)
  between operations  0.64 us (1%)
    pallas_call x1, Pallas kernels, exchange(): pl.pallas_call(comm_kernel, out_shape=(jax.ShapeDtypeStruct((2, W, 384),...  48 us
    pallas_call x1, Pallas kernels, expand(): pl.pallas_call(expand_kernel, out_shape=(jax.ShapeDtypeStruct((2, 768, W)...  4.73 us

profile of v3, /device:TPU:1, one launch (start us, length us, event | category | flops | bytes accessed | tf_op | source)
XLA Modules:
  0.0 53.4 jit_solution(14462468240156068817)
XLA Ops:
  0.6 48.0 %exchange.1 = (f32[2,256,384]{2,1,0:T(8,128)}, f32[2,384,256]{2,1,0:T(8,128)}, f32[2,384,128]{2,1,0:T(8,128)}) custom-call(s32[2,48]{1,0:T(2,128)} %lists.3, bf16[768,768]{1,0:T(8,128)(2,1)} %a_hbm.1, bf16[2,384,256]{2,1,0:T(8,128)(2,1)} %f_hbm.1), custom_call_target="tpu_custom_call" | custom-call | tf_op jit(solution)/shard_map/exchange/pallas_call | solution.py:408
  48.7 4.7 %expand.1 = (f32[2,768,256]{2,1,0:T(8,128)}, f32[2,256,768]{2,1,0:T(8,128)}, f32[2,256,256]{2,1,0:T(8,128)}) custom-call(s32[2,48]{1,0:T(2,128)} %lists.3, f32[2,256,384]{2,1,0:T(8,128)} %get-tuple-element.6.pc, f32[2,384,256]{2,1,0:T(8,128)} %get-tuple-element.7.pr, f32[2,384,128]{2,1,0:T(8,128)} %get-tuple-element.8.dg, f32[2,256,256]{2,1,0:T(8,128)} %diag.1), custom_call_target="tpu_custom_call" | custom-call | tf_op jit(solution)/shard_map/expand/pallas_call | solution.py:497

commit v4 on v3

--- a/solution.py
+++ b/solution.py
@@ -46,7 +46,7 @@
     ld_sem, fs_send, fs_recv, on_send, on_recv, rs_send, rs_recv,
     ag_send, ag_recv, rl_send, rl_recv, tp_send, tp_recv, zs_send, zs_recv,
     ys_send, ys_recv, dr_send, dr_recv, dz_send, dz_recv,
-    dg_send, dg_recv, do_send, do_recv, out_sem,
+    dg_send, dg_recv, do_send, do_recv, out_sem, met_line, met_mate,
 ):
     r = lax.axis_index("row")
     c = lax.axis_index("col")
@@ -73,27 +73,15 @@
 
     barrier = pltpu.get_barrier_semaphore()
 
-    @pl.when(r != c)
-    def _():
-        pl.semaphore_signal(barrier, inc=1, device_id=(c, r), device_id_type=MESH)
-
-    def greet_z(d, carry):
-        zo = lax.rem(zh + d // 2, 4)
-        pl.semaphore_signal(
-            barrier, inc=1, device_id=(lax.rem(d, 2) * 8 + lax.rem(r, 8), zo * 4 + y), device_id_type=MESH
-        )
-        return carry
-
-    lax.fori_loop(2, 8, greet_z, 0)
-
-    def greet_y(d, carry):
-        yo = lax.rem(y + d // 4, 4)
-        pl.semaphore_signal(
-            barrier, inc=1, device_id=(zl * 8 + lax.rem(d, 4) * 2 + k, zh * 4 + yo), device_id_type=MESH
-        )
-        return carry
-
-    lax.fori_loop(4, 16, greet_y, 0)
+    def line_y(d):
+        return zh * 4 + lax.rem(y + d, 4)
+
+    def line_z(d):
+        return lax.rem(zh + d, 4) * 4 + y
+
+    for d in range(1, 4):
+        pl.semaphore_signal(barrier, inc=1, device_id=(r, line_z(d)), device_id_type=MESH)
+        pl.semaphore_signal(barrier, inc=1, device_id=(r, line_y(d)), device_id_type=MESH)
 
     def greet(d, carry):
         pl.semaphore_signal(barrier, inc=1, device_id=(lax.rem(r + d, 16), c), device_id_type=MESH)
@@ -124,7 +112,10 @@
 
     partial(1 - k)
 
-    pl.semaphore_wait(barrier, jnp.where(r == c, 33, 34))
+    pl.semaphore_wait(barrier, 21)
+
+    for d in range(1, 4):
+        pl.semaphore_signal(met_line, inc=1, device_id=(r, line_y(d)), device_id_type=MESH)
 
     swap = rcopy(pp.at[1 - k], half, on_send, on_recv, mate, c)
     swap.start()
@@ -145,7 +136,10 @@
         fp[...] = f_v[k, pl.ds(pl.multiple_of(j * PIECE, PIECE), PIECE), :]
 
     partial(k)
+    pl.semaphore_wait(met_line, 3)
+    pl.semaphore_signal(met_mate, inc=1, device_id=(mate, c), device_id_type=MESH)
     swap.wait_recv()
+    pl.semaphore_wait(met_mate, 1)
 
     pp[k] = pp[k] + half[...]
 
@@ -218,19 +212,6 @@
 
     lax.fori_loop(1, CHIPS, ag_start, 0)
 
-    def rl_copy(s, slot):
-        return rcopy(pcv.at[s, slot], pcv.at[s, slot], rl_send.at[slot], rl_recv.at[slot], mate, c)
-
-    rl_copy(k, j).start()
-
-    def relay(d, carry):
-        o = chip(CHIPS - d)
-        ag_copy(d, o).wait_recv()
-        rl_copy(k, o).start()
-        return carry
-
-    lax.fori_loop(1, CHIPS, relay, 0)
-
     def dr_add(d, acc):
         o = around(16 - d)
         dr_copy(d, o).wait_recv()
@@ -251,12 +232,6 @@
 
     lax.fori_loop(1, 8, dz_start, 0)
 
-    def line_y(d):
-        return zh * 4 + lax.rem(y + d, 4)
-
-    def line_z(d):
-        return lax.rem(zh + d, 4) * 4 + y
-
     @pl.when(r != c)
     def _():
         rcopy(pcv.at[k, j], prv.at[here], tp_send, tp_recv, c, r).wait_recv()
@@ -280,11 +255,18 @@
     for d in range(1, 4):
         ys_copy(d, zh, c).start()
 
-    for d in range(1, 4):
-        o = lax.rem(zh + 4 - d, 4)
-        zs_copy(d, o * 4 + y).wait_recv()
-        for e in range(1, 4):
-            ys_copy(e, o, o * 4 + y).start()
+    def rl_copy(s, slot):
+        return rcopy(pcv.at[s, slot], pcv.at[s, slot], rl_send.at[slot], rl_recv.at[slot], mate, c)
+
+    rl_copy(k, j).start()
+
+    def relay(d, carry):
+        o = chip(CHIPS - d)
+        ag_copy(d, o).wait_recv()
+        rl_copy(k, o).start()
+        return carry
+
+    lax.fori_loop(1, CHIPS, relay, 0)
 
     def dz_wait(d, carry):
         dz_copy(d, lax.rem(z + 8 - d, 8)).wait_recv()
@@ -310,6 +292,12 @@
     lax.fori_loop(1, 16, dg_start, 0)
     do_copy(k, q).start()
 
+    for d in range(1, 4):
+        o = lax.rem(zh + 4 - d, 4)
+        zs_copy(d, o * 4 + y).wait_recv()
+        for e in range(1, 4):
+            ys_copy(e, o, o * 4 + y).start()
+
     for d in range(8):
         rl_copy(1 - k, d).wait_recv()
 
@@ -323,7 +311,7 @@
     lax.fori_loop(0, 16, open_pc, 0)
     for s in range(2):
         for p in range(3):
-            pct[s, :, p * BS : p * BS + BS] = jnp.transpose(pcf[s, p * BS : p * BS + BS, :])
+            pct[s, p] = jnp.transpose(pcf[s, p * BS : p * BS + BS, :])
     out_pc = pltpu.make_async_copy(pct, pc, out_sem.at[0])
     out_pc.start()
     for w in range(4):
@@ -408,7 +396,7 @@
     return pl.pallas_call(
         comm_kernel,
         out_shape=(
-            jax.ShapeDtypeStruct((2, W, 384), F32),
+            jax.ShapeDtypeStruct((2, 3, W, BS), F32),
             jax.ShapeDtypeStruct((2, 384, W), F32),
             jax.ShapeDtypeStruct((2, 384, 128), F32),
         ),
@@ -430,11 +418,12 @@
             pltpu.VMEM((2, 384, 128), F32),
             pltpu.VMEM((2, 384, W), F32),
             pltpu.VMEM((2, 384, W), F32),
-            pltpu.VMEM((2, W, 384), F32),
+            pltpu.VMEM((2, 3, W, BS), F32),
             dma((2,)), dma((16,)), dma, dma, dma, dma((8,)), dma((8,)),
             dma((8,)), dma((8,)), dma((8,)), dma((8,)), dma, dma, dma((4,)), dma((4,)),
             dma((4, 4)), dma((4, 4)), dma((16,)), dma((16,)), dma((8,)), dma((8,)),
             dma((16,)), dma((16,)), dma((16,)), dma((16,)), dma((3,)),
+            pltpu.SemaphoreType.REGULAR, pltpu.SemaphoreType.REGULAR,
         ],
         compiler_params=pltpu.CompilerParams(collective_id=0, has_side_effects=True),
         name="exchange",
@@ -462,7 +451,7 @@
     for s in range(2):
         for p in range(3):
             loads[0, s, p] = begin(pr.at[s, p * BS : p * BS + BS, :], row_in.at[s, p], r_sem.at[s, p])
-            loads[1, s, p] = begin(pc.at[s, :, p * BS : p * BS + BS], col_in.at[s, p], c_sem.at[s, p])
+            loads[1, s, p] = begin(pc.at[s, p], col_in.at[s, p], c_sem.at[s, p])
     zero[...] = jnp.zeros_like(zero)
     row_at = {}
     col_at = {}

time: 53.6 us -> 52.6 us (0.981)
  Pallas kernels: 52.8 us -> 51.8 us
    pallas_call x1, Pallas kernels: 48 us -> 47.1 us  [exchange(): pl.pallas_call(comm_kernel, out_shape=(jax.ShapeDtypeStruct((2, 3, W, BS)...]
where the time goes in v4:
time: 52.6 us; the launch traced here: 52.4 us
  Pallas kernels  51.8 us (98%)
  between operations  0.64 us (1%)
    pallas_call x1, Pallas kernels, exchange(): pl.pallas_call(comm_kernel, out_shape=(jax.ShapeDtypeStruct((2, 3, W, BS)...  47.1 us
    pallas_call x1, Pallas kernels, expand(): pl.pallas_call(expand_kernel, out_shape=(jax.ShapeDtypeStruct((2, 768, W)...  4.72 us

profile of v4, /device:TPU:1, one launch (start us, length us, event | category | flops | bytes accessed | tf_op | source)
XLA Modules:
  0.0 52.4 jit_solution(13070214258340222488)
XLA Ops:
  0.6 47.1 %exchange.1 = (f32[2,3,256,128]{3,2,1,0:T(8,128)}, f32[2,384,256]{2,1,0:T(8,128)}, f32[2,384,128]{2,1,0:T(8,128)}) custom-call(s32[2,48]{1,0:T(2,128)} %lists.3, bf16[768,768]{1,0:T(8,128)(2,1)} %a_hbm.1, bf16[2,384,256]{2,1,0:T(8,128)(2,1)} %f_hbm.1), custom_call_target="tpu_custom_call" | custom-call | tf_op jit(solution)/shard_map/exchange/pallas_call | solution.py:396
  47.7 4.7 %expand.1 = (f32[2,768,256]{2,1,0:T(8,128)}, f32[2,256,768]{2,1,0:T(8,128)}, f32[2,256,256]{2,1,0:T(8,128)}) custom-call(s32[2,48]{1,0:T(2,128)} %lists.3, f32[2,3,256,128]{3,2,1,0:T(8,128)} %get-tuple-element.6.pc, f32[2,384,256]{2,1,0:T(8,128)} %get-tuple-element.7.pr, f32[2,384,128]{2,1,0:T(8,128)} %get-tuple-element.8.dg, f32[2,256,256]{2,1,0:T(8,128)} %diag.1), custom_call_target="tpu_custom_call" | custom-call | tf_op jit(solution)/shard_map/expand/pallas_call | solution.py:486

commit v5 on v4

--- a/solution.py
+++ b/solution.py
@@ -40,11 +40,24 @@
     return coded[PIECE * half : PIECE * half + PIECE, :].astype(jnp.int32).astype(F32) * step
 
 
+def encode_rows(part):
+    most = jnp.max(jnp.abs(part), axis=-2, keepdims=True)
+    level = jnp.clip(jnp.ceil(8.0 * jnp.log2(jnp.maximum(most, 1e-30))), -800.0, 1000.0)
+    coded = jnp.round(part * (jnp.exp2(level * -0.125) * TOP)).astype(jnp.int32)
+    steps = jnp.broadcast_to(level, part.shape[:-2] + (8, 128)).astype(jnp.int32)
+    return jnp.concatenate([coded, steps], axis=-2).astype(jnp.int16)
+
+
+def decode_rows(coded):
+    wide = coded.astype(jnp.int32).astype(F32)
+    return wide[:24, :] * (jnp.exp2(wide[24:25, :] * 0.125) * (1.0 / TOP))
+
+
 def comm_kernel(
-    lists, a_hbm, f_hbm, pc, pr, dout,
-    a_v, f_v, asel, fp, pp, pcv, prv, half, rs, dp, dr, dz, dg, pcf, prf, pct,
+    lists_hbm, a_hbm, f_hbm, pc, pr, dout, lists,
+    a_v, f_v, asel, fp, pp, pcv, prv, half, rs, dp, dpc, dr, dz, dg, dgf, pcf, prf, pct,
     ld_sem, fs_send, fs_recv, on_send, on_recv, rs_send, rs_recv,
-    ag_send, ag_recv, rl_send, rl_recv, tp_send, tp_recv, zs_send, zs_recv,
+    ag_send, ag_recv, rl_send, rl_recv, tp_send, tp_recv,
     ys_send, ys_recv, dr_send, dr_recv, dz_send, dz_recv,
     dg_send, dg_recv, do_send, do_recv, out_sem, met_line, met_mate,
 ):
@@ -89,10 +102,13 @@
 
     lax.fori_loop(1, 16, greet, 0)
 
+    load_l = pltpu.make_async_copy(lists_hbm, lists, ld_sem.at[2])
+    load_l.start()
     load_a = pltpu.make_async_copy(a_hbm, a_v, ld_sem.at[0])
     load_f = pltpu.make_async_copy(f_hbm, f_v, ld_sem.at[1])
     load_a.start()
     load_f.start()
+    load_l.wait()
     load_a.wait()
     load_f.wait()
 
@@ -170,6 +186,8 @@
     dp[128:256, :] = top[:, 128:]
     dp[256:384, :] = dot_t(right, high[:, 128:]) + dot_t(right, low[:, 128:])
 
+    dpc[...] = encode_rows(dp[...].reshape(16, 24, 128))
+
     def around(d):
         return lax.rem(q + d, 16)
 
@@ -179,7 +197,7 @@
     def dr_copy(d, slot):
         o = around(d)
         return rcopy(
-            dp.at[rows24(o)], dr.at[slot], dr_send.at[o], dr_recv.at[slot],
+            dpc.at[o], dr.at[slot], dr_send.at[o], dr_recv.at[slot],
             zl * 8 + (o // 4) * 2 + k, zh * 4 + lax.rem(o, 4),
         )
 
@@ -192,32 +210,29 @@
     pcv[k, j] = encode(total)
 
     mine = k * CHIPS + j
-    here = ck * CHIPS + cj
-    cross = rcopy(pcv.at[k, j], prv.at[mine], tp_send, tp_recv, c, r)
-
-    @pl.when(r != c)
-    def _():
-        cross.start()
-
-    @pl.when(r == c)
-    def _():
-        prv[mine] = encode(total)
-
-    def ag_copy(d, slot):
-        return rcopy(pcv.at[k, slot], pcv.at[k, slot], ag_send.at[chip(d)], ag_recv.at[slot], 2 * chip(d) + k, c)
-
-    def ag_start(d, carry):
-        ag_copy(d, j).start()
-        return carry
-
-    lax.fori_loop(1, CHIPS, ag_start, 0)
+
+    def cross_copy(w):
+        return rcopy(pcv.at[k, j], prv.at[mine], tp_send.at[w], tp_recv.at[mine], c, w * 4 + lax.rem(r, 4))
+
+    def is_self(w):
+        return jnp.logical_and(r == c, w * 4 + lax.rem(r, 4) == c)
+
+    for w in range(4):
+
+        @pl.when(jnp.logical_not(is_self(w)))
+        def _():
+            cross_copy(w).start()
+
+        @pl.when(is_self(w))
+        def _():
+            prv[mine] = pcv[k, j]
 
     def dr_add(d, acc):
         o = around(16 - d)
         dr_copy(d, o).wait_recv()
-        return acc + dr[o]
-
-    dz[z] = lax.fori_loop(1, 16, dr_add, dp[rows24(q), :])
+        return acc + decode_rows(dr[o])
+
+    dz[z] = encode_rows(lax.fori_loop(1, 16, dr_add, dp[rows24(q), :]))
 
     def dz_copy(d, slot):
         o = lax.rem(z + d, 8)
@@ -232,19 +247,17 @@
 
     lax.fori_loop(1, 8, dz_start, 0)
 
-    @pl.when(r != c)
-    def _():
-        rcopy(pcv.at[k, j], prv.at[here], tp_send, tp_recv, c, r).wait_recv()
+    def ag_copy(d, slot):
+        return rcopy(pcv.at[k, slot], pcv.at[k, slot], ag_send.at[chip(d)], ag_recv.at[slot], 2 * chip(d) + k, c)
+
+    def ag_start(d, carry):
+        ag_copy(d, j).start()
+        return carry
+
+    lax.fori_loop(1, CHIPS, ag_start, 0)
 
     def slot_of(col):
         return lax.rem(col, 2) * CHIPS + col // 2
-
-    def zs_copy(d, col):
-        slot = slot_of(col)
-        return rcopy(prv.at[slot], prv.at[slot], zs_send.at[lax.rem(zh + d, 4)], zs_recv.at[col // 4], r, line_z(d))
-
-    for d in range(1, 4):
-        zs_copy(d, c).start()
 
     def ys_copy(d, w, col):
         slot = slot_of(col)
@@ -252,8 +265,15 @@
             prv.at[slot], prv.at[slot], ys_send.at[w, lax.rem(y + d, 4)], ys_recv.at[w, lax.rem(col, 4)], r, line_y(d)
         )
 
-    for d in range(1, 4):
-        ys_copy(d, zh, c).start()
+    for w in range(4):
+        slot = slot_of(w * 4 + y)
+
+        @pl.when(jnp.logical_not(jnp.logical_and(r == c, w == zh)))
+        def _():
+            rcopy(pcv.at[k, j], prv.at[slot], tp_send.at[w], tp_recv.at[slot], c, c).wait_recv()
+
+        for d in range(1, 4):
+            ys_copy(d, w, w * 4 + y).start()
 
     def rl_copy(s, slot):
         return rcopy(pcv.at[s, slot], pcv.at[s, slot], rl_send.at[slot], rl_recv.at[slot], mate, c)
@@ -273,17 +293,18 @@
         return carry
 
     lax.fori_loop(1, 8, dz_wait, 0)
-    dg[k, rows24(q), :] = ((dz[0] + dz[1]) + (dz[2] + dz[3])) + ((dz[4] + dz[5]) + (dz[6] + dz[7]))
+    both = [decode_rows(dz[2 * i]) + decode_rows(dz[2 * i + 1]) for i in range(4)]
+    dg[k, q] = encode_rows((both[0] + both[1]) + (both[2] + both[3]))
 
     def dg_copy(d, slot):
         o = around(d)
         return rcopy(
-            dg.at[k, rows24(slot)], dg.at[k, rows24(slot)], dg_send.at[o], dg_recv.at[slot],
+            dg.at[k, slot], dg.at[k, slot], dg_send.at[o], dg_recv.at[slot],
             zl * 8 + (o // 4) * 2 + k, zh * 4 + lax.rem(o, 4),
         )
 
     def do_copy(s, slot):
-        return rcopy(dg.at[s, rows24(slot)], dg.at[s, rows24(slot)], do_send.at[slot], do_recv.at[slot], mate, c)
+        return rcopy(dg.at[s, slot], dg.at[s, slot], do_send.at[slot], do_recv.at[slot], mate, c)
 
     def dg_start(d, carry):
         dg_copy(d, q).start()
@@ -291,12 +312,6 @@
 
     lax.fori_loop(1, 16, dg_start, 0)
     do_copy(k, q).start()
-
-    for d in range(1, 4):
-        o = lax.rem(zh + 4 - d, 4)
-        zs_copy(d, o * 4 + y).wait_recv()
-        for e in range(1, 4):
-            ys_copy(e, o, o * 4 + y).start()
 
     for d in range(8):
         rl_copy(1 - k, d).wait_recv()
@@ -333,23 +348,28 @@
         o = around(16 - d)
         dg_copy(d, o).wait_recv()
         do_copy(k, o).start()
-        return carry
-
+        dgf[k, rows24(o), :] = decode_rows(dg[k, o])
+        return carry
+
+    dgf[k, rows24(q), :] = decode_rows(dg[k, q])
     lax.fori_loop(1, 16, dg_relay, 0)
 
     def do_wait(d, carry):
         do_copy(1 - k, d).wait_recv()
+        dgf[1 - k, rows24(d), :] = decode_rows(dg[1 - k, d])
         return carry
 
     lax.fori_loop(0, 16, do_wait, 0)
-    out_d = pltpu.make_async_copy(dg, dout, out_sem.at[2])
+    out_d = pltpu.make_async_copy(dgf, dout, out_sem.at[2])
     out_d.start()
 
     swap.wait_send()
 
-    @pl.when(r != c)
-    def _():
-        cross.wait_send()
+    for w in range(4):
+
+        @pl.when(jnp.logical_not(is_self(w)))
+        def _():
+            cross_copy(w).wait_send()
 
     @pl.when(r == c)
     def _():
@@ -369,7 +389,6 @@
     for d in range(CHIPS):
         rl_copy(k, d).wait_send()
     for d in range(1, 4):
-        zs_copy(d, c).wait_send()
         for w in range(4):
             ys_copy(d, w, w * 4 + y).wait_send()
 
@@ -400,9 +419,10 @@
             jax.ShapeDtypeStruct((2, 384, W), F32),
             jax.ShapeDtypeStruct((2, 384, 128), F32),
         ),
-        in_specs=[pl.BlockSpec(memory_space=pltpu.SMEM), hbm, hbm],
+        in_specs=[hbm, hbm, hbm],
         out_specs=(hbm, hbm, hbm),
         scratch_shapes=[
+            pltpu.SMEM((2, 48), jnp.int32),
             pltpu.VMEM((768, 768), BF16),
             pltpu.VMEM((2, 384, W), BF16),
             pltpu.VMEM((384, 384), BF16),
@@ -413,14 +433,16 @@
             pltpu.VMEM((CHIPS, PIECE, W), F32),
             pltpu.VMEM((CHIPS, PIECE, W), F32),
             pltpu.VMEM((384, 128), F32),
-            pltpu.VMEM((16, 24, 128), F32),
-            pltpu.VMEM((8, 24, 128), F32),
+            pltpu.VMEM((16, 32, 128), jnp.int16),
+            pltpu.VMEM((16, 32, 128), jnp.int16),
+            pltpu.VMEM((8, 32, 128), jnp.int16),
+            pltpu.VMEM((2, 16, 32, 128), jnp.int16),
             pltpu.VMEM((2, 384, 128), F32),
             pltpu.VMEM((2, 384, W), F32),
             pltpu.VMEM((2, 384, W), F32),
             pltpu.VMEM((2, 3, W, BS), F32),
-            dma((2,)), dma((16,)), dma, dma, dma, dma((8,)), dma((8,)),
-            dma((8,)), dma((8,)), dma((8,)), dma((8,)), dma, dma, dma((4,)), dma((4,)),
+            dma((3,)), dma((16,)), dma, dma, dma, dma((8,)), dma((8,)),
+            dma((8,)), dma((8,)), dma((8,)), dma((8,)), dma((4,)), dma((16,)),
             dma((4, 4)), dma((4, 4)), dma((16,)), dma((16,)), dma((8,)), dma((8,)),
             dma((16,)), dma((16,)), dma((16,)), dma((16,)), dma((3,)),
             pltpu.SemaphoreType.REGULAR, pltpu.SemaphoreType.REGULAR,
@@ -431,7 +453,7 @@
 
 
 def expand_kernel(
-    lists, pc, pr, dg, diag, column, mirror, diagonal, col_in, row_in, dg_in, diag_in, zero, d_out,
+    lists_hbm, pc, pr, dg, diag, column, mirror, diagonal, lists, col_in, row_in, dg_in, diag_in, zero, d_out,
     r_sem, c_sem, d_sem, z_sem, o_sem,
 ):
     r = lax.axis_index("row")
@@ -446,6 +468,7 @@
     def span(block):
         return pl.ds(pl.multiple_of(block * BS, BS), BS)
 
+    load_l = begin(lists_hbm, lists, d_sem.at[3])
     loads_d = [begin(dg, dg_in, d_sem.at[0]), begin(diag, diag_in, d_sem.at[1])]
     loads = {}
     for s in range(2):
@@ -453,6 +476,7 @@
             loads[0, s, p] = begin(pr.at[s, p * BS : p * BS + BS, :], row_in.at[s, p], r_sem.at[s, p])
             loads[1, s, p] = begin(pc.at[s, p], col_in.at[s, p], c_sem.at[s, p])
     zero[...] = jnp.zeros_like(zero)
+    load_l.wait()
     row_at = {}
     col_at = {}
     for s in range(2):
@@ -490,16 +514,17 @@
             jax.ShapeDtypeStruct((2, W, 768), F32),
             jax.ShapeDtypeStruct((2, W, W), F32),
         ),
-        in_specs=[pl.BlockSpec(memory_space=pltpu.SMEM)] + [hbm] * 4,
+        in_specs=[hbm] * 5,
         out_specs=(hbm, hbm, hbm),
         scratch_shapes=[
+            pltpu.SMEM((2, 48), jnp.int32),
             pltpu.VMEM((2, 3, W, BS), F32),
             pltpu.VMEM((2, 3, BS, W), F32),
             pltpu.VMEM((2, 384, 128), F32),
             pltpu.VMEM((2, W, W), F32),
             pltpu.VMEM((W, W), F32),
             pltpu.VMEM((2, W, W), F32),
-            dma((2, 3)), dma((2, 3)), dma((3,)), dma((2, 2, 3)), dma((2, 2, 3)),
+            dma((2, 3)), dma((2, 3)), dma((4,)), dma((2, 2, 3)), dma((2, 2, 3)),
         ],
         name="expand",
     )(block_lists, col_packed, row_packed, upper, diag_inverse)

time: 52.6 us -> 46.2 us (0.88)
  Pallas kernels: 51.8 us -> 45.4 us
    pallas_call x1, Pallas kernels: 47.1 us -> 42 us  [exchange(): pl.pallas_call(comm_kernel, out_shape=(jax.ShapeDtypeStruct((2, 3, W, BS)...]
    pallas_call x1, Pallas kernels: 4.72 us -> 3.42 us  [expand(): pl.pallas_call(expand_kernel, out_shape=(jax.ShapeDtypeStruct((2, 768, W)...]
where the time goes in v5:
time: 46.2 us; the launch traced here: 46 us
  Pallas kernels  45.4 us (98%)
  between operations  0.64 us (1%)
    pallas_call x1, Pallas kernels, exchange(): pl.pallas_call(comm_kernel, out_shape=(jax.ShapeDtypeStruct((2, 3, W, BS)...  42 us
    pallas_call x1, Pallas kernels, expand(): pl.pallas_call(expand_kernel, out_shape=(jax.ShapeDtypeStruct((2, 768, W)...  3.42 us

profile of v5, /device:TPU:1, one launch (start us, length us, event | category | flops | bytes accessed | tf_op | source)
XLA Modules:
  0.0 46.0 jit_solution(8149303543375847125)
XLA Ops:
  0.6 42.0 %exchange.1 = (f32[2,3,256,128]{3,2,1,0:T(8,128)}, f32[2,384,256]{2,1,0:T(8,128)}, f32[2,384,128]{2,1,0:T(8,128)}) custom-call(s32[2,48]{1,0:T(2,128)} %lists_hbm.3, bf16[768,768]{1,0:T(8,128)(2,1)} %a_hbm.1, bf16[2,384,256]{2,1,0:T(8,128)(2,1)} %f_hbm.1), custom_call_target="tpu_custom_call" | custom-call | tf_op jit(solution)/shard_map/exchange/pallas_call | solution.py:415
  42.6 3.4 %expand.1 = (f32[2,768,256]{2,1,0:T(8,128)}, f32[2,256,768]{2,1,0:T(8,128)}, f32[2,256,256]{2,1,0:T(8,128)}) custom-call(s32[2,48]{1,0:T(2,128)} %lists_hbm.3, f32[2,3,256,128]{3,2,1,0:T(8,128)} %get-tuple-element.6.pc, f32[2,384,256]{2,1,0:T(8,128)} %get-tuple-element.7.pr, f32[2,384,128]{2,1,0:T(8,128)} %get-tuple-element.8.dg, f32[2,256,256]{2,1,0:T(8,128)} %diag.1), custom_call_target="tpu_custom_call" | custom-call | tf_op jit(solution)/shard_map/expand/pallas_call | solution.py:510

commit v6 on v5

--- a/solution.py
+++ b/solution.py
@@ -54,12 +54,12 @@
 
 
 def comm_kernel(
-    lists_hbm, a_hbm, f_hbm, pc, pr, dout, lists,
-    a_v, f_v, asel, fp, pp, pcv, prv, half, rs, dp, dpc, dr, dz, dg, dgf, pcf, prf, pct,
+    lists_hbm, a_hbm, f_hbm, diag_hbm, column, mirror, diagonal, lists, diag,
+    a_v, f_v, asel, fp, pp, pcv, prv, half, rs, dp, dpc, dr, dz, dg, dgf, pcf, prf,
     ld_sem, fs_send, fs_recv, on_send, on_recv, rs_send, rs_recv,
     ag_send, ag_recv, rl_send, rl_recv, tp_send, tp_recv,
     ys_send, ys_recv, dr_send, dr_recv, dz_send, dz_recv,
-    dg_send, dg_recv, do_send, do_recv, out_sem, met_line, met_mate,
+    dg_send, dg_recv, do_send, do_recv, met_line, met_mate,
 ):
     r = lax.axis_index("row")
     c = lax.axis_index("col")
@@ -104,6 +104,8 @@
 
     load_l = pltpu.make_async_copy(lists_hbm, lists, ld_sem.at[2])
     load_l.start()
+    load_d = pltpu.make_async_copy(diag_hbm, diag, ld_sem.at[3])
+    load_d.start()
     load_a = pltpu.make_async_copy(a_hbm, a_v, ld_sem.at[0])
     load_f = pltpu.make_async_copy(f_hbm, f_v, ld_sem.at[1])
     load_a.start()
@@ -326,9 +328,10 @@
     lax.fori_loop(0, 16, open_pc, 0)
     for s in range(2):
         for p in range(3):
-            pct[s, p] = jnp.transpose(pcf[s, p * BS : p * BS + BS, :])
-    out_pc = pltpu.make_async_copy(pct, pc, out_sem.at[0])
-    out_pc.start()
+            at = lists[s, c * 3 + p] - 2 * (c * 3 + p)
+            block = jnp.transpose(pcf[s, p * BS : p * BS + BS, :])
+            mirror[s, :, 2 * p * BS : 2 * p * BS + BS] = jnp.where(at == 0, block, 0.0)
+            mirror[s, :, 2 * p * BS + BS : 2 * p * BS + 2 * BS] = jnp.where(at == 0, 0.0, block)
     for w in range(4):
         for d in range(1, 4):
             ys_copy(d, w, w * 4 + lax.rem(y + 4 - d, 4)).wait_recv()
@@ -341,8 +344,13 @@
         return carry
 
     lax.fori_loop(0, 16, open_pr, 0)
-    out_pr = pltpu.make_async_copy(prf, pr, out_sem.at[1])
-    out_pr.start()
+    for s in range(2):
+        for p in range(3):
+            at = lists[s, r * 3 + p] - 2 * (r * 3 + p)
+            block = prf[s, p * BS : p * BS + BS, :]
+            column[s, 2 * p * BS : 2 * p * BS + BS, :] = jnp.where(at == 0, block, 0.0)
+            column[s, 2 * p * BS + BS : 2 * p * BS + 2 * BS, :] = jnp.where(at == 0, 0.0, block)
+    load_d.wait()
 
     def dg_relay(d, carry):
         o = around(16 - d)
@@ -360,8 +368,12 @@
         return carry
 
     lax.fori_loop(0, 16, do_wait, 0)
-    out_d = pltpu.make_async_copy(dgf, dout, out_sem.at[2])
-    out_d.start()
+    for s in range(2):
+        upper = dgf[s, 128:256, :]
+        diagonal[s, 0:128, 0:128] = diag[s, 0:128, 0:128] + dgf[s, 0:128, :]
+        diagonal[s, 0:128, 128:256] = diag[s, 0:128, 128:256] + upper
+        diagonal[s, 128:256, 0:128] = diag[s, 128:256, 0:128] + jnp.transpose(upper)
+        diagonal[s, 128:256, 128:256] = diag[s, 128:256, 128:256] + dgf[s, 256:384, :]
 
     swap.wait_send()
 
@@ -404,25 +416,20 @@
         return carry
 
     lax.fori_loop(0, 16, drain_relay, 0)
-    out_pc.wait()
-    out_pr.wait()
-    out_d.wait()
-
-
-def exchange(blocks_inverse, factor_rows, block_lists):
+
+
+def exchange(blocks_inverse, factor_rows, block_lists, diag_inverse):
     dma = pltpu.SemaphoreType.DMA
     hbm = pl.BlockSpec(memory_space=pl.ANY)
+    vmem = pl.BlockSpec(memory_space=pltpu.VMEM)
     return pl.pallas_call(
         comm_kernel,
-        out_shape=(
-            jax.ShapeDtypeStruct((2, 3, W, BS), F32),
-            jax.ShapeDtypeStruct((2, 384, W), F32),
-            jax.ShapeDtypeStruct((2, 384, 128), F32),
-        ),
-        in_specs=[hbm, hbm, hbm],
-        out_specs=(hbm, hbm, hbm),
+        out_shape=(pltpu.VMEM((2, 768, W), F32), pltpu.VMEM((2, W, 768), F32), pltpu.VMEM((2, W, W), F32)),
+        in_specs=[hbm] * 4,
+        out_specs=(vmem, vmem, vmem),
         scratch_shapes=[
             pltpu.SMEM((2, 48), jnp.int32),
+            pltpu.VMEM((2, W, W), F32),
             pltpu.VMEM((768, 768), BF16),
             pltpu.VMEM((2, 384, W), BF16),
             pltpu.VMEM((384, 384), BF16),
@@ -440,101 +447,44 @@
             pltpu.VMEM((2, 384, 128), F32),
             pltpu.VMEM((2, 384, W), F32),
             pltpu.VMEM((2, 384, W), F32),
-            pltpu.VMEM((2, 3, W, BS), F32),
-            dma((3,)), dma((16,)), dma, dma, dma, dma((8,)), dma((8,)),
+            dma((4,)), dma((16,)), dma, dma, dma, dma((8,)), dma((8,)),
             dma((8,)), dma((8,)), dma((8,)), dma((8,)), dma((4,)), dma((16,)),
             dma((4, 4)), dma((4, 4)), dma((16,)), dma((16,)), dma((8,)), dma((8,)),
-            dma((16,)), dma((16,)), dma((16,)), dma((16,)), dma((3,)),
+            dma((16,)), dma((16,)), dma((16,)), dma((16,)),
             pltpu.SemaphoreType.REGULAR, pltpu.SemaphoreType.REGULAR,
         ],
-        compiler_params=pltpu.CompilerParams(collective_id=0, has_side_effects=True),
+        compiler_params=pltpu.CompilerParams(collective_id=0, has_side_effects=True, vmem_limit_bytes=63300000),
         name="exchange",
-    )(block_lists, blocks_inverse, factor_rows)
-
-
-def expand_kernel(
-    lists_hbm, pc, pr, dg, diag, column, mirror, diagonal, lists, col_in, row_in, dg_in, diag_in, zero, d_out,
-    r_sem, c_sem, d_sem, z_sem, o_sem,
-):
-    r = lax.axis_index("row")
-    c = lax.axis_index("col")
-    stores = []
-
-    def begin(src, dst, sem):
-        copy = pltpu.make_async_copy(src, dst, sem)
+    )(block_lists, blocks_inverse, factor_rows, diag_inverse)
+
+
+def store_kernel(column, mirror, diagonal, column_out, mirror_out, diagonal_out, sems):
+    copies = [
+        pltpu.make_async_copy(diagonal, diagonal_out, sems.at[0]),
+        pltpu.make_async_copy(column, column_out, sems.at[1]),
+        pltpu.make_async_copy(mirror, mirror_out, sems.at[2]),
+    ]
+    for copy in copies:
         copy.start()
-        return copy
-
-    def span(block):
-        return pl.ds(pl.multiple_of(block * BS, BS), BS)
-
-    load_l = begin(lists_hbm, lists, d_sem.at[3])
-    loads_d = [begin(dg, dg_in, d_sem.at[0]), begin(diag, diag_in, d_sem.at[1])]
-    loads = {}
-    for s in range(2):
-        for p in range(3):
-            loads[0, s, p] = begin(pr.at[s, p * BS : p * BS + BS, :], row_in.at[s, p], r_sem.at[s, p])
-            loads[1, s, p] = begin(pc.at[s, p], col_in.at[s, p], c_sem.at[s, p])
-    zero[...] = jnp.zeros_like(zero)
-    load_l.wait()
-    row_at = {}
-    col_at = {}
-    for s in range(2):
-        for p in range(3):
-            row_at[s, p] = lists[s, r * 3 + p] - 2 * (r * 3 + p)
-            col_at[s, p] = lists[s, c * 3 + p] - 2 * (c * 3 + p)
-            stores.append(begin(zero.at[0:128, :], column.at[s, span(2 * p + 1 - row_at[s, p])], z_sem.at[0, s, p]))
-            stores.append(begin(zero.at[:, 0:128], mirror.at[s, :, span(2 * p + 1 - col_at[s, p])], z_sem.at[1, s, p]))
-    for load in loads_d:
-        load.wait()
-    for s in range(2):
-        upper = dg_in[s, 128:256, :]
-        d_out[s, 0:128, 0:128] = diag_in[s, 0:128, 0:128] + dg_in[s, 0:128, :]
-        d_out[s, 0:128, 128:256] = diag_in[s, 0:128, 128:256] + upper
-        d_out[s, 128:256, 0:128] = diag_in[s, 128:256, 0:128] + jnp.transpose(upper)
-        d_out[s, 128:256, 128:256] = diag_in[s, 128:256, 128:256] + dg_in[s, 256:384, :]
-    stores.append(begin(d_out, diagonal, d_sem.at[2]))
-    for s in range(2):
-        for p in range(3):
-            loads[0, s, p].wait()
-            stores.append(begin(row_in.at[s, p], column.at[s, span(2 * p + row_at[s, p])], o_sem.at[0, s, p]))
-            loads[1, s, p].wait()
-            stores.append(begin(col_in.at[s, p], mirror.at[s, :, span(2 * p + col_at[s, p])], o_sem.at[1, s, p]))
-    for store in stores:
-        store.wait()
-
-
-def expand(block_lists, col_packed, row_packed, upper, diag_inverse):
-    dma = pltpu.SemaphoreType.DMA
+    for copy in copies:
+        copy.wait()
+
+
+def store(column, mirror, diagonal):
     hbm = pl.BlockSpec(memory_space=pl.ANY)
     return pl.pallas_call(
-        expand_kernel,
-        out_shape=(
-            jax.ShapeDtypeStruct((2, 768, W), F32),
-            jax.ShapeDtypeStruct((2, W, 768), F32),
-            jax.ShapeDtypeStruct((2, W, W), F32),
-        ),
-        in_specs=[hbm] * 5,
+        store_kernel,
+        out_shape=tuple(jax.ShapeDtypeStruct(a.shape, F32) for a in (column, mirror, diagonal)),
+        in_specs=[pl.BlockSpec(memory_space=pltpu.VMEM)] * 3,
         out_specs=(hbm, hbm, hbm),
-        scratch_shapes=[
-            pltpu.SMEM((2, 48), jnp.int32),
-            pltpu.VMEM((2, 3, W, BS), F32),
-            pltpu.VMEM((2, 3, BS, W), F32),
-            pltpu.VMEM((2, 384, 128), F32),
-            pltpu.VMEM((2, W, W), F32),
-            pltpu.VMEM((W, W), F32),
-            pltpu.VMEM((2, W, W), F32),
-            dma((2, 3)), dma((2, 3)), dma((4,)), dma((2, 2, 3)), dma((2, 2, 3)),
-        ],
-        name="expand",
-    )(block_lists, col_packed, row_packed, upper, diag_inverse)
+        scratch_shapes=[pltpu.SemaphoreType.DMA((3,))],
+        compiler_params=pltpu.CompilerParams(vmem_limit_bytes=8 << 20),
+        name="store",
+    )(column, mirror, diagonal)
 
 
 def local(blocks_inverse, factor_rows, block_lists, diag_inverse):
-    col_packed, row_packed, upper = exchange(blocks_inverse, factor_rows, block_lists)
-    return expand(
-        block_lists, col_packed, row_packed, upper, diag_inverse
-    )
+    return store(*exchange(blocks_inverse, factor_rows, block_lists, diag_inverse))
 
 
 def solution(mesh):

time: 46.2 us -> 44.4 us (0.961)
  Pallas kernels: 45.4 us -> 43.6 us
    pallas_call x2, Pallas kernels: 45.4 us -> 43.6 us  [the longest x1 41.8 us: exchange(): pl.pallas_call(comm_kernel, out_shape=(pltpu.VMEM((2, 768, W), F32), pltp...]
where the time goes in v6:
time: 44.4 us; the launch traced here: 44.3 us
  Pallas kernels  43.6 us (98%)
  between operations  0.64 us (1%)
    pallas_call x1, Pallas kernels, exchange(): pl.pallas_call(comm_kernel, out_shape=(pltpu.VMEM((2, 768, W), F32), pltp...  41.8 us
    pallas_call x1, Pallas kernels, store(): pl.pallas_call(store_kernel, out_shape=tuple((jax.ShapeDtypeStruct(a.shap...  1.86 us

profile of v6, /device:TPU:1, one launch (start us, length us, event | category | flops | bytes accessed | tf_op | source)
XLA Modules:
  0.0 44.3 jit_solution(1048244300320053854)
XLA Ops:
  0.6 41.8 %exchange.1 = (f32[2,768,256]{2,1,0:T(8,128)S(1)}, f32[2,256,768]{2,1,0:T(8,128)S(1)}, f32[2,256,256]{2,1,0:T(8,128)S(1)}) custom-call(s32[2,48]{1,0:T(2,128)} %lists_hbm.1, bf16[768,768]{1,0:T(8,128)(2,1)} %a_hbm.1, bf16[2,384,256]{2,1,0:T(8,128)(2,1)} %f_hbm.1, f32[2,256,256]{2,1,0:T(8,128)} %diag_hbm.1), custom_call_target="tpu_custom_call" | custom-call | tf_op jit(solution)/shard_map/exchange/pallas_call | solution.py:425
  42.4 1.9 %store.1 = (f32[2,768,256]{2,1,0:T(8,128)}, f32[2,256,768]{2,1,0:T(8,128)}, f32[2,256,256]{2,1,0:T(8,128)}) custom-call(f32[2,768,256]{2,1,0:T(8,128)S(1)} %get-tuple-element.6.column, f32[2,256,768]{2,1,0:T(8,128)S(1)} %get-tuple-element.7.mirror, f32[2,256,256]{2,1,0:T(8,128)S(1)} %get-tuple-element.8.diagonal), custom_call_target="tpu_custom_call" | custom-call | tf_op jit(solution)/shard_map/store/pallas_call | solution.py:475

commit v7 on v6

--- a/solution.py
+++ b/solution.py
@@ -55,7 +55,7 @@
 
 def comm_kernel(
     lists_hbm, a_hbm, f_hbm, diag_hbm, column, mirror, diagonal, lists, diag,
-    a_v, f_v, asel, fp, pp, pcv, prv, half, rs, dp, dpc, dr, dz, dg, dgf, pcf, prf,
+    a_v, f_v, asel, fp, pp, pcv, prv, half, rs, qc, dp, dpc, dr, dz, dg, dgf, pcf, prf,
     ld_sem, fs_send, fs_recv, on_send, on_recv, rs_send, rs_recv,
     ag_send, ag_recv, rl_send, rl_recv, tp_send, tp_recv,
     ys_send, ys_recv, dr_send, dr_recv, dz_send, dz_recv,
@@ -135,8 +135,14 @@
     for d in range(1, 4):
         pl.semaphore_signal(met_line, inc=1, device_id=(r, line_y(d)), device_id_type=MESH)
 
-    swap = rcopy(pp.at[1 - k], half, on_send, on_recv, mate, c)
-    swap.start()
+    def swap_copy(o):
+        return rcopy(pp.at[1 - k, o], half.at[o], on_send.at[o], on_recv.at[o], mate, c)
+
+    def swap_start(d, carry):
+        swap_copy(chip(d)).start()
+        return carry
+
+    lax.fori_loop(1, CHIPS + 1, swap_start, 0)
 
     def fcopy(o):
         return rcopy(
@@ -156,25 +162,28 @@
     partial(k)
     pl.semaphore_wait(met_line, 3)
     pl.semaphore_signal(met_mate, inc=1, device_id=(mate, c), device_id_type=MESH)
-    swap.wait_recv()
     pl.semaphore_wait(met_mate, 1)
 
-    pp[k] = pp[k] + half[...]
 
     def rs_copy(d, slot):
         o = chip(d)
-        return rcopy(pp.at[k, o], rs.at[slot], rs_send.at[o], rs_recv.at[slot], 2 * o + k, c)
+        return rcopy(qc.at[o], rs.at[slot], rs_send.at[o], rs_recv.at[slot], 2 * o + k, c)
 
     def rs_start(d, carry):
+        o = chip(d)
+        swap_copy(o).wait_recv()
+        qc[o] = encode(pp[k, o] + half[o])
         rs_copy(d, j).start()
         return carry
 
     lax.fori_loop(1, CHIPS, rs_start, 0)
-    total = pp[k, j]
+    swap_copy(j).wait_recv()
+    total = pp[k, j] + half[j]
     for d in range(1, CHIPS):
         o = chip(CHIPS - d)
         rs_copy(d, o).wait_recv()
-        total = total + rs[o]
+        coded = rs[o]
+        total = total - jnp.concatenate([decode_half(coded, 0), decode_half(coded, 1)], axis=1)
     @pl.when(r != c)
     def _():
         fcopy(r).wait_recv()
@@ -375,7 +384,11 @@
         diagonal[s, 128:256, 0:128] = diag[s, 128:256, 0:128] + jnp.transpose(upper)
         diagonal[s, 128:256, 128:256] = diag[s, 128:256, 128:256] + dgf[s, 256:384, :]
 
-    swap.wait_send()
+    def swap_drain(d, carry):
+        swap_copy(d).wait_send()
+        return carry
+
+    lax.fori_loop(0, CHIPS, swap_drain, 0)
 
     for w in range(4):
 
@@ -438,7 +451,8 @@
             pltpu.VMEM((2, CHIPS, CODED, 128), jnp.int16),
             pltpu.VMEM((16, CODED, 128), jnp.int16),
             pltpu.VMEM((CHIPS, PIECE, W), F32),
-            pltpu.VMEM((CHIPS, PIECE, W), F32),
+            pltpu.VMEM((CHIPS, CODED, 128), jnp.int16),
+            pltpu.VMEM((CHIPS, CODED, 128), jnp.int16),
             pltpu.VMEM((384, 128), F32),
             pltpu.VMEM((16, 32, 128), jnp.int16),
             pltpu.VMEM((16, 32, 128), jnp.int16),
@@ -447,7 +461,7 @@
             pltpu.VMEM((2, 384, 128), F32),
             pltpu.VMEM((2, 384, W), F32),
             pltpu.VMEM((2, 384, W), F32),
-            dma((4,)), dma((16,)), dma, dma, dma, dma((8,)), dma((8,)),
+            dma((4,)), dma((16,)), dma, dma((8,)), dma((8,)), dma((8,)), dma((8,)),
             dma((8,)), dma((8,)), dma((8,)), dma((8,)), dma((4,)), dma((16,)),
             dma((4, 4)), dma((4, 4)), dma((16,)), dma((16,)), dma((8,)), dma((8,)),
             dma((16,)), dma((16,)), dma((16,)), dma((16,)),

time: 44.4 us -> 42.8 us (0.964)
  Pallas kernels: 43.6 us -> 42.1 us
    pallas_call x1, Pallas kernels: 41.8 us -> 40.2 us  [exchange(): pl.pallas_call(comm_kernel, out_shape=(pltpu.VMEM((2, 768, W), F32), pltp...]
where the time goes in v7:
time: 42.8 us; the launch traced here: 42.7 us
  Pallas kernels  42.1 us (98%)
  between operations  0.64 us (1%)
    pallas_call x1, Pallas kernels, exchange(): pl.pallas_call(comm_kernel, out_shape=(pltpu.VMEM((2, 768, W), F32), pltp...  40.2 us
    pallas_call x1, Pallas kernels, store(): pl.pallas_call(store_kernel, out_shape=tuple((jax.ShapeDtypeStruct(a.shap...  1.86 us

profile of v7, /device:TPU:1, one launch (start us, length us, event | category | flops | bytes accessed | tf_op | source)
XLA Modules:
  0.0 42.7 jit_solution(382027734253135200)
XLA Ops:
  0.6 40.2 %exchange.1 = (f32[2,768,256]{2,1,0:T(8,128)S(1)}, f32[2,256,768]{2,1,0:T(8,128)S(1)}, f32[2,256,256]{2,1,0:T(8,128)S(1)}) custom-call(s32[2,48]{1,0:T(2,128)} %lists_hbm.1, bf16[768,768]{1,0:T(8,128)(2,1)} %a_hbm.1, bf16[2,384,256]{2,1,0:T(8,128)(2,1)} %f_hbm.1, f32[2,256,256]{2,1,0:T(8,128)} %diag_hbm.1), custom_call_target="tpu_custom_call" | custom-call | tf_op jit(solution)/shard_map/exchange/pallas_call | solution.py:438
  40.8 1.9 %store.1 = (f32[2,768,256]{2,1,0:T(8,128)}, f32[2,256,768]{2,1,0:T(8,128)}, f32[2,256,256]{2,1,0:T(8,128)}) custom-call(f32[2,768,256]{2,1,0:T(8,128)S(1)} %get-tuple-element.6.column, f32[2,256,768]{2,1,0:T(8,128)S(1)} %get-tuple-element.7.mirror, f32[2,256,256]{2,1,0:T(8,128)S(1)} %get-tuple-element.8.diagonal), custom_call_target="tpu_custom_call" | custom-call | tf_op jit(solution)/shard_map/store/pallas_call | solution.py:489

commit v8 on v7

--- a/solution.py
+++ b/solution.py
@@ -18,6 +18,15 @@
 
 def dot_t(a, b):
     return lax.dot_general(a, b, (((0,), (0,)), ((), ())), preferred_element_type=F32)
+
+
+def ring(d, n):
+    return min(d, n - d)
+
+
+PLANE = sorted(((i, e) for i in range(4) for e in range(4) if i + e), key=lambda t: ring(t[0], 4) + ring(t[1], 4))
+GROUP = sorted(((i, e) for i in range(2) for e in range(4) if i + e), key=lambda t: t[0] + ring(t[1], 4))
+RING_Z = sorted(range(1, 8), key=lambda d: ring(d, 8))
 
 
 def encode(piece):
@@ -59,7 +68,7 @@
     ld_sem, fs_send, fs_recv, on_send, on_recv, rs_send, rs_recv,
     ag_send, ag_recv, rl_send, rl_recv, tp_send, tp_recv,
     ys_send, ys_recv, dr_send, dr_recv, dz_send, dz_recv,
-    dg_send, dg_recv, do_send, do_recv, met_line, met_mate,
+    dg_send, dg_recv, do_send, do_recv, met_a, met_b, met_c,
 ):
     r = lax.axis_index("row")
     c = lax.axis_index("col")
@@ -78,6 +87,18 @@
     def chip(d):
         return lax.rem(j + d, CHIPS)
 
+    def group_to(off):
+        return lax.rem(zl + off[0], 2) * 4 + lax.rem(x + off[1], 4)
+
+    def group_from(off):
+        return lax.rem(zl + off[0], 2) * 4 + lax.rem(x + 4 - off[1], 4)
+
+    def plane_to(off):
+        return lax.rem(x + off[0], 4) * 4 + lax.rem(y + off[1], 4)
+
+    def plane_from(off):
+        return lax.rem(x + 4 - off[0], 4) * 4 + lax.rem(y + 4 - off[1], 4)
+
     def rcopy(src, dst, ssem, rsem, row, col):
         return pltpu.make_async_remote_copy(
             src_ref=src, dst_ref=dst, send_sem=ssem, recv_sem=rsem,
@@ -92,8 +113,9 @@
     def line_z(d):
         return lax.rem(zh + d, 4) * 4 + y
 
+    for d in (1, 3):
+        pl.semaphore_signal(barrier, inc=1, device_id=(r, line_z(d)), device_id_type=MESH)
     for d in range(1, 4):
-        pl.semaphore_signal(barrier, inc=1, device_id=(r, line_z(d)), device_id_type=MESH)
         pl.semaphore_signal(barrier, inc=1, device_id=(r, line_y(d)), device_id_type=MESH)
 
     def greet(d, carry):
@@ -130,19 +152,19 @@
 
     partial(1 - k)
 
-    pl.semaphore_wait(barrier, 21)
-
+    pl.semaphore_wait(barrier, 20)
+
+    for d in (1, 3):
+        pl.semaphore_signal(met_a, inc=1, device_id=(r, line_z(d)), device_id_type=MESH)
     for d in range(1, 4):
-        pl.semaphore_signal(met_line, inc=1, device_id=(r, line_y(d)), device_id_type=MESH)
+        pl.semaphore_signal(met_a, inc=1, device_id=(r, line_y(d)), device_id_type=MESH)
 
     def swap_copy(o):
         return rcopy(pp.at[1 - k, o], half.at[o], on_send.at[o], on_recv.at[o], mate, c)
 
-    def swap_start(d, carry):
-        swap_copy(chip(d)).start()
-        return carry
-
-    lax.fori_loop(1, CHIPS + 1, swap_start, 0)
+    for off in GROUP[::-1]:
+        swap_copy(group_to(off)).start()
+    swap_copy(j).start()
 
     def fcopy(o):
         return rcopy(
@@ -160,30 +182,33 @@
         fp[...] = f_v[k, pl.ds(pl.multiple_of(j * PIECE, PIECE), PIECE), :]
 
     partial(k)
-    pl.semaphore_wait(met_line, 3)
-    pl.semaphore_signal(met_mate, inc=1, device_id=(mate, c), device_id_type=MESH)
-    pl.semaphore_wait(met_mate, 1)
-
-
-    def rs_copy(d, slot):
-        o = chip(d)
+
+    def rs_copy(o, slot):
         return rcopy(qc.at[o], rs.at[slot], rs_send.at[o], rs_recv.at[slot], 2 * o + k, c)
 
-    def rs_start(d, carry):
-        o = chip(d)
+    for off in GROUP[::-1]:
+        o = group_to(off)
         swap_copy(o).wait_recv()
         qc[o] = encode(pp[k, o] + half[o])
-        rs_copy(d, j).start()
-        return carry
-
-    lax.fori_loop(1, CHIPS, rs_start, 0)
+        rs_copy(o, j).start()
+    pl.semaphore_wait(met_a, 5)
+    for d in range(1, 4):
+        pl.semaphore_signal(met_b, inc=1, device_id=(r, line_y(d)), device_id_type=MESH)
     swap_copy(j).wait_recv()
     total = pp[k, j] + half[j]
-    for d in range(1, CHIPS):
-        o = chip(CHIPS - d)
-        rs_copy(d, o).wait_recv()
+    pl.semaphore_wait(met_b, 3)
+
+    def tell(d, carry):
+        pl.semaphore_signal(met_c, inc=1, device_id=(lax.rem(r + d, 16), c), device_id_type=MESH)
+        return carry
+
+    lax.fori_loop(1, 16, tell, 0)
+    for off in GROUP:
+        o = group_from(off)
+        rs_copy(o, o).wait_recv()
         coded = rs[o]
         total = total - jnp.concatenate([decode_half(coded, 0), decode_half(coded, 1)], axis=1)
+
     @pl.when(r != c)
     def _():
         fcopy(r).wait_recv()
@@ -205,20 +230,17 @@
     def rows24(o):
         return pl.ds(pl.multiple_of(o * 24, 8), 24)
 
-    def dr_copy(d, slot):
-        o = around(d)
+    def dr_copy(o, slot):
         return rcopy(
             dpc.at[o], dr.at[slot], dr_send.at[o], dr_recv.at[slot],
             zl * 8 + (o // 4) * 2 + k, zh * 4 + lax.rem(o, 4),
         )
 
-    def dr_start(d, carry):
-        dr_copy(d, q).start()
-        return carry
-
-    lax.fori_loop(1, 16, dr_start, 0)
+    for off in PLANE[::-1]:
+        dr_copy(plane_to(off), q).start()
 
     pcv[k, j] = encode(total)
+    pl.semaphore_wait(met_c, 15)
 
     mine = k * CHIPS + j
 
@@ -238,12 +260,12 @@
         def _():
             prv[mine] = pcv[k, j]
 
-    def dr_add(d, acc):
-        o = around(16 - d)
-        dr_copy(d, o).wait_recv()
-        return acc + decode_rows(dr[o])
-
-    dz[z] = encode_rows(lax.fori_loop(1, 16, dr_add, dp[rows24(q), :]))
+    acc = dp[rows24(q), :]
+    for off in PLANE:
+        o = plane_from(off)
+        dr_copy(o, o).wait_recv()
+        acc = acc + decode_rows(dr[o])
+    dz[z] = encode_rows(acc)
 
     def dz_copy(d, slot):
         o = lax.rem(z + d, 8)
@@ -252,11 +274,8 @@
             lax.rem(o, 2) * 8 + lax.rem(r, 8), (o // 2) * 4 + y,
         )
 
-    def dz_start(d, carry):
+    for d in RING_Z[::-1]:
         dz_copy(d, z).start()
-        return carry
-
-    lax.fori_loop(1, 8, dz_start, 0)
 
     def ag_copy(d, slot):
         return rcopy(pcv.at[k, slot], pcv.at[k, slot], ag_send.at[chip(d)], ag_recv.at[slot], 2 * chip(d) + k, c)
@@ -307,8 +326,7 @@
     both = [decode_rows(dz[2 * i]) + decode_rows(dz[2 * i + 1]) for i in range(4)]
     dg[k, q] = encode_rows((both[0] + both[1]) + (both[2] + both[3]))
 
-    def dg_copy(d, slot):
-        o = around(d)
+    def dg_copy(o, slot):
         return rcopy(
             dg.at[k, slot], dg.at[k, slot], dg_send.at[o], dg_recv.at[slot],
             zl * 8 + (o // 4) * 2 + k, zh * 4 + lax.rem(o, 4),
@@ -317,11 +335,8 @@
     def do_copy(s, slot):
         return rcopy(dg.at[s, slot], dg.at[s, slot], do_send.at[slot], do_recv.at[slot], mate, c)
 
-    def dg_start(d, carry):
-        dg_copy(d, q).start()
-        return carry
-
-    lax.fori_loop(1, 16, dg_start, 0)
+    for off in PLANE[::-1]:
+        dg_copy(plane_to(off), q).start()
     do_copy(k, q).start()
 
     for d in range(8):
@@ -361,22 +376,16 @@
             column[s, 2 * p * BS + BS : 2 * p * BS + 2 * BS, :] = jnp.where(at == 0, 0.0, block)
     load_d.wait()
 
-    def dg_relay(d, carry):
-        o = around(16 - d)
-        dg_copy(d, o).wait_recv()
+    dgf[k, rows24(q), :] = decode_rows(dg[k, q])
+    for off in PLANE:
+        o = plane_from(off)
+        dg_copy(o, o).wait_recv()
         do_copy(k, o).start()
         dgf[k, rows24(o), :] = decode_rows(dg[k, o])
-        return carry
-
-    dgf[k, rows24(q), :] = decode_rows(dg[k, q])
-    lax.fori_loop(1, 16, dg_relay, 0)
-
-    def do_wait(d, carry):
-        do_copy(1 - k, d).wait_recv()
-        dgf[1 - k, rows24(d), :] = decode_rows(dg[1 - k, d])
-        return carry
-
-    lax.fori_loop(0, 16, do_wait, 0)
+    for off in [(0, 0)] + PLANE:
+        o = plane_from(off)
+        do_copy(1 - k, o).wait_recv()
+        dgf[1 - k, rows24(o), :] = decode_rows(dg[1 - k, o])
     for s in range(2):
         upper = dgf[s, 128:256, :]
         diagonal[s, 0:128, 0:128] = diag[s, 0:128, 0:128] + dgf[s, 0:128, :]
@@ -405,7 +414,7 @@
         lax.fori_loop(1, 16, scattered, 0)
 
     def drain(d, carry):
-        rs_copy(d, j).wait_send()
+        rs_copy(chip(d), j).wait_send()
         ag_copy(d, j).wait_send()
         dz_copy(d, z).wait_send()
         return carry
@@ -418,8 +427,8 @@
             ys_copy(d, w, w * 4 + y).wait_send()
 
     def drain_plane(d, carry):
-        dr_copy(d, q).wait_send()
-        dg_copy(d, q).wait_send()
+        dr_copy(around(d), q).wait_send()
+        dg_copy(around(d), q).wait_send()
         return carry
 
     lax.fori_loop(1, 16, drain_plane, 0)
@@ -465,7 +474,7 @@
             dma((8,)), dma((8,)), dma((8,)), dma((8,)), dma((4,)), dma((16,)),
             dma((4, 4)), dma((4, 4)), dma((16,)), dma((16,)), dma((8,)), dma((8,)),
             dma((16,)), dma((16,)), dma((16,)), dma((16,)),
-            pltpu.SemaphoreType.REGULAR, pltpu.SemaphoreType.REGULAR,
+            pltpu.SemaphoreType.REGULAR, pltpu.SemaphoreType.REGULAR, pltpu.SemaphoreType.REGULAR,
         ],
         compiler_params=pltpu.CompilerParams(collective_id=0, has_side_effects=True, vmem_limit_bytes=63300000),
         name="exchange",

time: 42.8 us -> 40 us (0.935)
  Pallas kernels: 42.1 us -> 39.2 us
    pallas_call x1, Pallas kernels: 40.2 us -> 37.4 us  [exchange(): pl.pallas_call(comm_kernel, out_shape=(pltpu.VMEM((2, 768, W), F32), pltp...]
where the time goes in v8:
time: 40 us; the launch traced here: 39.9 us
  Pallas kernels  39.2 us (98%)
  between operations  0.64 us (2%)
    pallas_call x1, Pallas kernels, exchange(): pl.pallas_call(comm_kernel, out_shape=(pltpu.VMEM((2, 768, W), F32), pltp...  37.4 us
    pallas_call x1, Pallas kernels, store(): pl.pallas_call(store_kernel, out_shape=tuple((jax.ShapeDtypeStruct(a.shap...  1.86 us

profile of v8, /device:TPU:1, one launch (start us, length us, event | category | flops | bytes accessed | tf_op | source)
XLA Modules:
  0.0 39.9 jit_solution(3851749172427106248)
XLA Ops:
  0.6 37.4 %exchange.1 = (f32[2,768,256]{2,1,0:T(8,128)S(1)}, f32[2,256,768]{2,1,0:T(8,128)S(1)}, f32[2,256,256]{2,1,0:T(8,128)S(1)}) custom-call(s32[2,48]{1,0:T(2,128)} %lists_hbm.1, bf16[768,768]{1,0:T(8,128)(2,1)} %a_hbm.1, bf16[2,384,256]{2,1,0:T(8,128)(2,1)} %f_hbm.1, f32[2,256,256]{2,1,0:T(8,128)} %diag_hbm.1), custom_call_target="tpu_custom_call" | custom-call | tf_op jit(solution)/shard_map/exchange/pallas_call | solution.py:447
  38.0 1.9 %store.1 = (f32[2,768,256]{2,1,0:T(8,128)}, f32[2,256,768]{2,1,0:T(8,128)}, f32[2,256,256]{2,1,0:T(8,128)}) custom-call(f32[2,768,256]{2,1,0:T(8,128)S(1)} %get-tuple-element.6.column, f32[2,256,768]{2,1,0:T(8,128)S(1)} %get-tuple-element.7.mirror, f32[2,256,256]{2,1,0:T(8,128)S(1)} %get-tuple-element.8.diagonal), custom_call_target="tpu_custom_call" | custom-call | tf_op jit(solution)/shard_map/store/pallas_call | solution.py:498

commit v9 on v8

--- a/solution.py
+++ b/solution.py
@@ -305,6 +305,31 @@
         for d in range(1, 4):
             ys_copy(d, w, w * 4 + y).start()
 
+    def dz_wait(d, carry):
+        dz_copy(d, lax.rem(z + 8 - d, 8)).wait_recv()
+        return carry
+
+    lax.fori_loop(1, 8, dz_wait, 0)
+    both = [decode_rows(dz[2 * i]) + decode_rows(dz[2 * i + 1]) for i in range(4)]
+    dg[k, q] = encode_rows((both[0] + both[1]) + (both[2] + both[3]))
+
+    def dg_copy(o, slot):
+        return rcopy(
+            dg.at[k, slot], dg.at[k, slot], dg_send.at[o], dg_recv.at[slot],
+            zl * 8 + (o // 4) * 2 + k, zh * 4 + lax.rem(o, 4),
+        )
+
+    def do_copy(o, s, slot):
+        return rcopy(
+            dg.at[s, slot], dg.at[s, slot], do_send.at[o], do_recv.at[slot],
+            zl * 8 + (o // 4) * 2 + 1 - k, zh * 4 + lax.rem(o, 4),
+        )
+
+    for off in PLANE[::-1]:
+        dg_copy(plane_to(off), q).start()
+        do_copy(plane_to(off), k, q).start()
+    do_copy(q, k, q).start()
+
     def rl_copy(s, slot):
         return rcopy(pcv.at[s, slot], pcv.at[s, slot], rl_send.at[slot], rl_recv.at[slot], mate, c)
 
@@ -317,27 +342,6 @@
         return carry
 
     lax.fori_loop(1, CHIPS, relay, 0)
-
-    def dz_wait(d, carry):
-        dz_copy(d, lax.rem(z + 8 - d, 8)).wait_recv()
-        return carry
-
-    lax.fori_loop(1, 8, dz_wait, 0)
-    both = [decode_rows(dz[2 * i]) + decode_rows(dz[2 * i + 1]) for i in range(4)]
-    dg[k, q] = encode_rows((both[0] + both[1]) + (both[2] + both[3]))
-
-    def dg_copy(o, slot):
-        return rcopy(
-            dg.at[k, slot], dg.at[k, slot], dg_send.at[o], dg_recv.at[slot],
-            zl * 8 + (o // 4) * 2 + k, zh * 4 + lax.rem(o, 4),
-        )
-
-    def do_copy(s, slot):
-        return rcopy(dg.at[s, slot], dg.at[s, slot], do_send.at[slot], do_recv.at[slot], mate, c)
-
-    for off in PLANE[::-1]:
-        dg_copy(plane_to(off), q).start()
-    do_copy(k, q).start()
 
     for d in range(8):
         rl_copy(1 - k, d).wait_recv()
@@ -380,11 +384,10 @@
     for off in PLANE:
         o = plane_from(off)
         dg_copy(o, o).wait_recv()
-        do_copy(k, o).start()
         dgf[k, rows24(o), :] = decode_rows(dg[k, o])
     for off in [(0, 0)] + PLANE:
         o = plane_from(off)
-        do_copy(1 - k, o).wait_recv()
+        do_copy(o, 1 - k, o).wait_recv()
         dgf[1 - k, rows24(o), :] = decode_rows(dg[1 - k, o])
     for s in range(2):
         upper = dgf[s, 128:256, :]
@@ -434,7 +437,7 @@
     lax.fori_loop(1, 16, drain_plane, 0)
 
     def drain_relay(d, carry):
-        do_copy(k, d).wait_send()
+        do_copy(d, k, q).wait_send()
         return carry
 
     lax.fori_loop(0, 16, drain_relay, 0)

time: 40 us -> 39.2 us (0.980)
  Pallas kernels: 39.2 us -> 38.4 us
    pallas_call x1, Pallas kernels: 37.4 us -> 36.6 us  [exchange(): pl.pallas_call(comm_kernel, out_shape=(pltpu.VMEM((2, 768, W), F32), pltp...]
where the time goes in v9:
time: 39.2 us; the launch traced here: 39.1 us
  Pallas kernels  38.4 us (98%)
  between operations  0.64 us (2%)
    pallas_call x1, Pallas kernels, exchange(): pl.pallas_call(comm_kernel, out_shape=(pltpu.VMEM((2, 768, W), F32), pltp...  36.6 us
    pallas_call x1, Pallas kernels, store(): pl.pallas_call(store_kernel, out_shape=tuple((jax.ShapeDtypeStruct(a.shap...  1.86 us

profile of v9, /device:TPU:1, one launch (start us, length us, event | category | flops | bytes accessed | tf_op | source)
XLA Modules:
  0.0 39.1 jit_solution(2031564670083135686)
XLA Ops:
  0.6 36.6 %exchange.1 = (f32[2,768,256]{2,1,0:T(8,128)S(1)}, f32[2,256,768]{2,1,0:T(8,128)S(1)}, f32[2,256,256]{2,1,0:T(8,128)S(1)}) custom-call(s32[2,48]{1,0:T(2,128)} %lists_hbm.1, bf16[768,768]{1,0:T(8,128)(2,1)} %a_hbm.1, bf16[2,384,256]{2,1,0:T(8,128)(2,1)} %f_hbm.1, f32[2,256,256]{2,1,0:T(8,128)} %diag_hbm.1), custom_call_target="tpu_custom_call" | custom-call | tf_op jit(solution)/shard_map/exchange/pallas_call | solution.py:450
  37.2 1.9 %store.1 = (f32[2,768,256]{2,1,0:T(8,128)}, f32[2,256,768]{2,1,0:T(8,128)}, f32[2,256,256]{2,1,0:T(8,128)}) custom-call(f32[2,768,256]{2,1,0:T(8,128)S(1)} %get-tuple-element.6.column, f32[2,256,768]{2,1,0:T(8,128)S(1)} %get-tuple-element.7.mirror, f32[2,256,256]{2,1,0:T(8,128)S(1)} %get-tuple-element.8.diagonal), custom_call_target="tpu_custom_call" | custom-call | tf_op jit(solution)/shard_map/store/pallas_call | solution.py:501

commit v10 on v9

--- a/solution.py
+++ b/solution.py
@@ -277,15 +277,6 @@
     for d in RING_Z[::-1]:
         dz_copy(d, z).start()
 
-    def ag_copy(d, slot):
-        return rcopy(pcv.at[k, slot], pcv.at[k, slot], ag_send.at[chip(d)], ag_recv.at[slot], 2 * chip(d) + k, c)
-
-    def ag_start(d, carry):
-        ag_copy(d, j).start()
-        return carry
-
-    lax.fori_loop(1, CHIPS, ag_start, 0)
-
     def slot_of(col):
         return lax.rem(col, 2) * CHIPS + col // 2
 
@@ -304,6 +295,15 @@
 
         for d in range(1, 4):
             ys_copy(d, w, w * 4 + y).start()
+
+    def ag_copy(d, slot):
+        return rcopy(pcv.at[k, slot], pcv.at[k, slot], ag_send.at[chip(d)], ag_recv.at[slot], 2 * chip(d) + k, c)
+
+    def ag_start(d, carry):
+        ag_copy(d, j).start()
+        return carry
+
+    lax.fori_loop(1, CHIPS, ag_start, 0)
 
     def dz_wait(d, carry):
         dz_copy(d, lax.rem(z + 8 - d, 8)).wait_recv()

time: 39.2 us -> 39.2 us (level)
  no operation moved by 1% of the time
where the time goes in v10:
time: 39.2 us; the launch traced here: 39.1 us
  Pallas kernels  38.4 us (98%)
  between operations  0.64 us (2%)
    pallas_call x1, Pallas kernels, exchange(): pl.pallas_call(comm_kernel, out_shape=(pltpu.VMEM((2, 768, W), F32), pltp...  36.6 us
    pallas_call x1, Pallas kernels, store(): pl.pallas_call(store_kernel, out_shape=tuple((jax.ShapeDtypeStruct(a.shap...  1.86 us

profile of v10, /device:TPU:1, one launch (start us, length us, event | category | flops | bytes accessed | tf_op | source)
XLA Modules:
  0.0 39.1 jit_solution(14762674529238617847)
XLA Ops:
  0.6 36.6 %exchange.1 = (f32[2,768,256]{2,1,0:T(8,128)S(1)}, f32[2,256,768]{2,1,0:T(8,128)S(1)}, f32[2,256,256]{2,1,0:T(8,128)S(1)}) custom-call(s32[2,48]{1,0:T(2,128)} %lists_hbm.1, bf16[768,768]{1,0:T(8,128)(2,1)} %a_hbm.1, bf16[2,384,256]{2,1,0:T(8,128)(2,1)} %f_hbm.1, f32[2,256,256]{2,1,0:T(8,128)} %diag_hbm.1), custom_call_target="tpu_custom_call" | custom-call | tf_op jit(solution)/shard_map/exchange/pallas_call | solution.py:450
  37.2 1.9 %store.1 = (f32[2,768,256]{2,1,0:T(8,128)}, f32[2,256,768]{2,1,0:T(8,128)}, f32[2,256,256]{2,1,0:T(8,128)}) custom-call(f32[2,768,256]{2,1,0:T(8,128)S(1)} %get-tuple-element.6.column, f32[2,256,768]{2,1,0:T(8,128)S(1)} %get-tuple-element.7.mirror, f32[2,256,256]{2,1,0:T(8,128)S(1)} %get-tuple-element.8.diagonal), custom_call_target="tpu_custom_call" | custom-call | tf_op jit(solution)/shard_map/store/pallas_call | solution.py:501
